TPU v7x, 128 devices: a whole 4x4x4 slice. The times are simulated.
128 devices in a mesh: gx: 8 (over y, core), gy: 16 (over z, x).
Axes of the slice: x: 4, y: 4, z: 4, core: 2. Of those that a mesh axis runs over, the one named last changes fastest.
Arguments:
- elem_volume: float32 [294912], P(('gx', 'gy')), may hold values from 0.5 to 1.5
- elem_velocity: float32 [3, 294912], P(None, ('gx', 'gy')), may hold values from -6 to 6
- elem_energy: float32 [294912], P(('gx', 'gy')), may hold values from 0.3 to 3
- elem_mat: int32 [294912], P(('gx', 'gy')), may hold values from 0 to 7
- elem_dest: int32 [2304], P(('gx', 'gy')), may hold values from 0 to 127, as said below
- tile_slot: int32 [16384], P(('gx', 'gy')), may hold values from 0 to 255, as said below
- tile_cell: int32 [16384], P(('gx', 'gy')), may hold values from 0 to 1023
- tile_weight: bfloat16 [16384, 128, 128], P(('gx', 'gy')), may hold values from 0.00390625 to 0.01171875
- tile_count: int32 [128], P(('gx', 'gy')), may hold values from 32 to 128, as said below
- cell_state: float32 [12, 512, 32768], P(None, 'gx', 'gy'), may hold values from -4 to 4, as said below
- mat_props: float32 [2, 8], replicated, may hold values from 0.5 to 4
Outputs:
- remapped: float32 [12, 512, 32768], P(None, 'gx', 'gy')
- elem_pressure: bfloat16 [294912], P(('gx', 'gy'))
Inputs may be any that keep to these rules, and one draw needn't show every extreme that they name: `elem_dest`: each device sends exactly 2 of its blocks to each of the nine devices at offsets -1, 0, +1 along gx and along gy, wrapping at the ends, itself included. `tile_slot`: A value is source * 2 + rank of a block that was sent to this device; every block sent to a device is named by some tile below its count. `tile_count`: some device has all 128 tiles counted. `cell_state`: the volume and energy rows lie between 0.1 and 1; the three momentum rows are signed.
All inputs are finite; a program needn't handle non-finite values.
Results may differ from a plain program's by a relative error of at most 0.0024.
Values may be sent and summed in bfloat16 or wider, within the bound.
A program may use at most 192 MiB of HBM per device.

v0:
```python
import jax
import jax.numpy as jnp
from jax import lax
from jax.sharding import PartitionSpec as P

MAT = 8
NZ = 64
BLK = 128
CAP = 2


time_step = 0.8


def from_behind(value, axis, steps):
    count = lax.axis_size(axis)
    pairs = [(source, (source + steps) % count) for source in range(count)]
    return lax.ppermute(value, axis, pairs)


def with_halo(value, sides, width):
    for axis, dim in sides:
        size, length = (lax.axis_size(axis), value.shape[dim])
        up = [(i, (i + 1) % size) for i in range(size - 1)]
        down = [(j, i) for i, j in up]
        last = lax.slice_in_dim(value, length - width, length, axis=dim)
        leading = lax.slice_in_dim(value, 0, width, axis=dim)
        before = lax.ppermute(last, axis, up)
        after = lax.ppermute(leading, axis, down)
        value = jnp.concatenate([before, value, after], axis=dim)
    return value


def face_flux(q_lo, q_hi, u_lo, u_hi):
    speed = 0.5 * (u_lo + u_hi)
    return 0.5 * (speed * (q_lo + q_hi) - jnp.abs(speed) * (q_hi - q_lo))


def wrap_offset(diff, extent):
    value = (diff + extent) % extent
    return jnp.where(value == extent - 1, -1, value)


def neighbours(parcel, sign):
    lines = []
    for first in range(3):
        line = []
        for second in range(3):
            piece = parcel[first, second]
            if first != 1:
                piece = from_behind(piece, "gx", sign * (first - 1))
            if second != 1:
                piece = from_behind(piece, "gy", sign * (second - 1))
            line.append(piece)
        lines.append(jnp.stack(line))
    return jnp.stack(lines)


def per_device(
    elem_volume,
    elem_velocity,
    elem_energy,
    elem_mat,
    elem_dest,
    tile_slot,
    tile_cell,
    tile_weight,
    tile_count,
    cell_state,
    mat_props,
):
    grid_x = lax.axis_size("gx")
    grid_y = lax.axis_size("gy")
    pos_x = lax.axis_index("gx")
    pos_y = lax.axis_index("gy")
    n_blocks = elem_dest.shape[0]
    n_tiles = tile_weight.shape[0]
    count_q = cell_state.shape[0]
    width_x = cell_state.shape[1]
    width_y = cell_state.shape[2] // NZ
    n_cellblk = width_x * width_y * NZ // BLK
    density = mat_props[0]
    modulus = mat_props[1]
    onehot = (elem_mat[None, :] == jnp.arange(MAT, dtype=jnp.int32)[:, None]).astype(jnp.float32)
    mass_e = elem_volume * jnp.sum(onehot * density[:, None], axis=0)
    momentum = mass_e[None, :] * elem_velocity
    heat = (mass_e * elem_energy)[None, :]
    rows = jnp.concatenate([onehot * elem_volume[None, :], momentum, heat], axis=0).astype(
        jnp.bfloat16
    )
    n_rows = rows.shape[0]
    blocks = rows.reshape(n_rows, n_blocks, BLK).transpose(1, 0, 2)
    index = jnp.arange(n_blocks, dtype=jnp.int32)
    same = elem_dest[:, None] == elem_dest[None, :]
    rank = jnp.sum((same & (index[:, None] > index[None, :])).astype(jnp.int32), axis=1)
    near = (
        (wrap_offset(elem_dest // grid_y - pos_x, grid_x) + 1) * 3
        + wrap_offset(elem_dest % grid_y - pos_y, grid_y)
        + 1
    )
    outgoing = jnp.zeros((9 * CAP, n_rows, BLK), jnp.bfloat16).at[near * CAP + rank].set(blocks)
    incoming = neighbours(outgoing.reshape(3, 3, CAP, n_rows, BLK), 1)
    received = incoming.reshape(9 * CAP, n_rows, BLK)
    source = tile_slot // CAP
    step_x = wrap_offset(pos_x - source // grid_y, grid_x)
    step_y = wrap_offset(pos_y - source % grid_y, grid_y)
    local_slot = ((step_x + 1) * 3 + step_y + 1) * CAP + tile_slot % CAP
    n_slots = 9 * CAP
    tile_rows = jnp.take(received, local_slot, axis=0)
    valid = (jnp.arange(n_tiles, dtype=jnp.int32) < tile_count[0]).astype(jnp.float32)
    contrib = (
        jnp.einsum("trb,tbc->rtc", tile_rows, tile_weight, preferred_element_type=jnp.float32)
        * valid[None, :, None]
    )
    cell_pick = (tile_cell[None, :] == jnp.arange(n_cellblk, dtype=jnp.int32)[:, None]).astype(
        jnp.float32
    )
    dep = jnp.einsum("kt,rtc->rkc", cell_pick, contrib, precision=lax.Precision.HIGHEST)
    dep = dep.reshape(count_q, width_x, width_y, NZ)
    state = cell_state.reshape(count_q, width_x, width_y, NZ) + dep
    mass = 1.0 + jnp.sum(density[:, None, None, None] * state[:MAT], axis=0)
    speeds = jnp.stack([state[MAT] / mass, state[MAT + 1] / mass], axis=0)
    packed = jnp.concatenate([state, speeds], axis=0)
    framed = with_halo(packed.astype(jnp.bfloat16), (("gx", 1), ("gy", 2)), 1).astype(packed.dtype)
    along_x = framed[:, :, 1:-1]
    flux_x = face_flux(
        along_x[:count_q, :-1],
        along_x[:count_q, 1:],
        along_x[count_q : count_q + 1, :-1],
        along_x[count_q : count_q + 1, 1:],
    )
    along_y = framed[:, 1:-1]
    flux_y = face_flux(
        along_y[:count_q, :, :-1],
        along_y[:count_q, :, 1:],
        along_y[count_q + 1 : count_q + 2, :, :-1],
        along_y[count_q + 1 : count_q + 2, :, 1:],
    )
    fresh = state - time_step * (
        flux_x[:, 1:] - flux_x[:, :-1] + flux_y[:, :, 1:] - flux_y[:, :, :-1]
    )
    remapped = fresh.reshape(count_q, width_x, width_y * NZ)
    volumes = fresh[:MAT]
    pressure = (
        jnp.sum(modulus[:, None, None, None] * volumes * (1.0 + 0.5 * volumes), axis=0)
        + 0.4 * fresh[count_q - 1]
    )
    press_blocks = pressure.astype(jnp.bfloat16).reshape(n_cellblk, BLK)
    picked = jnp.take(press_blocks, tile_cell, axis=0)
    probe = jnp.stack([picked, jnp.ones_like(picked)], axis=1)
    both = (
        jnp.einsum("tec,tkc->tke", tile_weight, probe, preferred_element_type=jnp.float32)
        * valid[:, None, None]
    )
    slot_pick = (local_slot[None, :] == jnp.arange(n_slots, dtype=jnp.int32)[:, None]).astype(
        jnp.float32
    )
    sums = jnp.dot(
        slot_pick, both.reshape(n_tiles, 2 * BLK), precision=lax.Precision.HIGHEST
    ).reshape(n_slots, 2, BLK)
    answer = (sums[:, 0] / jnp.maximum(sums[:, 1], 1.0)).astype(jnp.bfloat16)
    returned = neighbours(answer.reshape(3, 3, CAP, BLK), -1).reshape(9 * CAP, BLK)
    mine = jnp.take(returned, near * CAP + rank, axis=0)
    return (remapped, mine.reshape(n_blocks * BLK))


def solution(mesh):
    placed = (
        P(("gx", "gy")),
        P(None, ("gx", "gy")),
        P(("gx", "gy")),
        P(("gx", "gy")),
        P(("gx", "gy")),
        P(("gx", "gy")),
        P(("gx", "gy")),
        P(("gx", "gy"), None, None),
        P(("gx", "gy")),
        P(None, "gx", "gy"),
        P(),
    )
    return jax.shard_map(
        per_device,
        mesh=mesh,
        in_specs=placed,
        out_specs=(P(None, "gx", "gy"), P(("gx", "gy"))),
        check_vma=False,
    )
```

profile of v0, /device:TPU:0, one launch (start us, length us, event | category | flops | bytes accessed | tf_op | source)
XLA Modules:
  0.0 214.2 jit_solution(11470580203144526105)
XLA Ops:
  0.6 0.9 convert_reduce_fusion
  1.5 0.8 slice_bitcast_fusion.18
  2.3 0.8 select_reduce_fusion
  3.1 0.7 fusion.25
  3.9 0.8 fusion.18
  4.6 0.7 select_convert_fusion
  6.1 1.5 scatter_fusion
  7.7 1.8 collective-permute-start.9
  9.5 1.5 collective-permute-start.6
  11.0 4.7 %collective-permute-start.5 = (bf16[2,12,128]{2,1,0:T(8,128)(2,1)S(1)}, bf16[2,12,128]{2,1,0:T(8,128)(2,1)S(1)}, u32[]{:S(2)}, u32[]{:S(2)}) collective-permute-start(bf16[2,12,128]{2,1,0:T(8,128)(2,1)S(1)} %get-tuple-element.26), channel_id=1, source_target_pairs={{0,15},{1,0},{2,1},{3,2},{4,3},{5,4},{6,5},{7,6},{8,7},{9,8},{10,9... | collective-permute-start | bytes 18440 | tf_op jit(solution)/shard_map/ppermute | solution.py:18
  16.4 0.7 compare_and_fusion.2
  17.2 11.4 %reshape.129 = f32[12,64,32,64]{3,2,1,0:T(8,128)} reshape(f32[12,64,2048]{2,1,0:T(8,128)} %param.20) | data formatting | bytes 12582912 | tf_op jit(solution)/shard_map/reshape | solution.py:120
  28.5 2.7 %collective-permute-start.3 = (bf16[2,12,128]{2,1,0:T(8,128)(2,1)S(1)}, bf16[2,12,128]{2,1,0:T(8,128)(2,1)S(1)}, u32[]{:S(2)}, u32[]{:S(2)}) collective-permute-start(bf16[2,12,128]{2,1,0:T(8,128)(2,1)S(1)} %get-tuple-element.27), channel_id=1, source_target_pairs={{0,112},{16,0},{32,16},{48,32},{64,48},{80,64},{96,80},{112,96},{1... | collective-permute-start | bytes 18440 | tf_op jit(solution)/shard_map/ppermute | solution.py:18
  31.3 5.3 %collective-permute-start.8 = (bf16[2,12,128]{2,1,0:T(8,128)(2,1)S(1)}, bf16[2,12,128]{2,1,0:T(8,128)(2,1)S(1)}, u32[]{:S(2)}, u32[]{:S(2)}) collective-permute-start(bf16[2,12,128]{2,1,0:T(8,128)(2,1)S(1)} %collective-permute-done.7), channel_id=1, source_target_pairs={{0,15},{1,0},{2,1},{3,2},{4,3},{5,4},{6,5},{7,6},{8,7},{9,8},{10,9... | collective-permute-start | bytes 18440 | tf_op jit(solution)/shard_map/ppermute | solution.py:18
  36.8 5.3 %collective-permute-start.1 = (bf16[2,12,128]{2,1,0:T(8,128)(2,1)S(1)}, bf16[2,12,128]{2,1,0:T(8,128)(2,1)S(1)}, u32[]{:S(2)}, u32[]{:S(2)}) collective-permute-start(bf16[2,12,128]{2,1,0:T(8,128)(2,1)S(1)} %collective-permute-done), channel_id=1, source_target_pairs={{0,15},{1,0},{2,1},{3,2},{4,3},{5,4},{6,5},{7,6},{8,7},{9,8},{10,9... | collective-permute-start | bytes 18440 | tf_op jit(solution)/shard_map/ppermute | solution.py:18
  42.1 1.6 collective-permute-done.4
  43.8 0.7 gather_fusion
  44.5 3.5 %fusion.3 = f32[12,128,128]{2,0,1:T(8,128)S(1)} fusion(bf16[128,128,128]{2,1,0:T(8,128)(2,1)} %param.18, f32[128]{0:T(128)S(1)} %get-tuple-element.40, bf16[128,12,128]{2,1,0:T(8,128)(2,1)S(1)} %gather_fusion, pred[128]{0:T(512)(128)(4,1)S(1)} %get-tuple-element.6), kind=kOutput, calls=%fused_computation.17 | convolution fusion | flops 50724864 | bytes 5374592 | tf_op jit(solution)/shard_map/trb,tbc->rtc/dot_general | solution.py:112
  47.9 4.6 %convolution_bitcast_fusion = f32[12,1024,128]{1,2,0:T(8,128)} fusion(f32[12,128,128]{2,0,1:T(8,128)S(1)} %fusion.3, s32[128]{0:T(128)S(1)} %copy-done.2), kind=kOutput, calls=%fused_computation.15 | convolution fusion | flops 2416050176 | bytes 7078400 | tf_op jit(solution)/shard_map/kt,rtc->rkc/dot_general | solution.py:118
  52.6 6.6 %copy.23 = f32[12,1024,128]{2,1,0:T(8,128)} copy(f32[12,1024,128]{1,2,0:T(8,128)} %convolution_bitcast_fusion) | data formatting | bytes 12582912 | tf_op jit(solution)/shard_map/kt,rtc->rkc/transpose | solution.py:118
  59.2 10.3 %reshape.132 = f32[12,64,32,64]{3,2,1,0:T(8,128)} reshape(f32[12,1024,128]{2,1,0:T(8,128)} %copy.23) | data formatting | bytes 12582912 | tf_op jit(solution)/shard_map/reshape | solution.py:119
  69.4 9.7 %fusion.44 = (bf16[12,64,32,64]{3,2,1,0:T(8,128)(2,1)S(1)}, f32[12,64,32,64]{3,2,1,0:T(8,128)S(1)}) fusion(f32[12,64,32,64]{3,2,1,0:T(8,128)} %reshape.129, f32[12,64,32,64]{3,2,1,0:T(8,128)} %reshape.132), kind=kLoop, calls=%fused_computation.157 | loop fusion | flops 3145728 | bytes 22020096 | tf_op jit(solution)/shard_map/convert
  79.2 1.2 fusion.2
  80.9 1.3 collective-permute-start.13
  82.2 3.0 %collective-permute-start.12 = (bf16[14,1,32,64]{3,2,1,0:T(8,128)(2,1)S(1)}, bf16[14,1,32,64]{3,2,1,0:T(8,128)(2,1)S(1)}, u32[]{:S(2)}, u32[]{:S(2)}) collective-permute-start(bf16[14,1,32,64]{3,2,1,0:T(8,128)(2,1)S(1)} %get-tuple-element.18), channel_id=1, source_target_pairs={{0,16},{16,32},{32,48},{48,64},{64,80},{80,96},{96,112},{1,17},{17... | collective-permute-start | bytes 172040 | tf_op jit(solution)/shard_map/ppermute | solution.py:28
  85.2 0.9 collective-permute-done.12
  86.1 2.4 %pad_maximum_fusion.4 = (bf16[14,66,1,64]{3,2,1,0:T(2,128)(2,1)S(1)}, bf16[14,66,1,64]{3,2,1,0:T(2,128)(2,1)S(1)}) fusion(bf16[14,1,32,64]{3,2,1,0:T(8,128)(2,1)S(1)} %collective-permute-done.13, bf16[14,1,32,64]{3,2,1,0:T(8,128)(2,1)S(1)} %collective-permute-done.12, bf16[1,64,32,64]{3,2,1,0:T(8,128)(2,1)S(1)} %get-tuple-element.15, ...), kind=kLoop, calls=%fused_computation.40 | loop fusion | flops 1182720 | bytes 4021248 | tf_op jit(solution)/shard_map/slice | solution.py:26
  88.5 1.3 collective-permute-start.15
  89.8 4.8 %collective-permute-start.14 = (bf16[14,66,1,64]{3,2,1,0:T(2,128)(2,1)S(1)}, bf16[14,66,1,64]{3,2,1,0:T(2,128)(2,1)S(1)}, u32[]{:S(2)}, u32[]{:S(2)}) collective-permute-start(bf16[14,66,1,64]{3,2,1,0:T(2,128)(2,1)S(1)} %get-tuple-element.16), channel_id=1, source_target_pairs={{0,1},{1,2},{2,3},{3,4},{4,5},{5,6},{6,7},{7,8},{8,9},{9,10},{10,1... | collective-permute-start | bytes 354824 | tf_op jit(solution)/shard_map/ppermute | solution.py:28
  94.6 8.6 %collective-permute-done.15 = bf16[14,66,1,64]{3,2,1,0:T(2,128)(2,1)S(1)} collective-permute-done((bf16[14,66,1,64]{3,2,1,0:T(2,128)(2,1)S(1)}, bf16[14,66,1,64]{3,2,1,0:T(2,128)(2,1)S(1)}, u32[]{:S(2)}, u32[]{:S(2)}) %collective-permute-start.15) | collective-permute-done | bytes 118304 | tf_op jit(solution)/shard_map/ppermute | solution.py:29
  103.2 1.7 collective-permute-done.14
  105.0 13.2 %maximum_convert_fusion = f32[14,66,34,64]{3,2,1,0:T(8,128)S(1)} fusion(bf16[14,66,1,64]{3,2,1,0:T(2,128)(2,1)S(1)} %collective-permute-done.15, bf16[14,1,32,64]{3,2,1,0:T(8,128)(2,1)S(1)} %collective-permute-done.13, bf16[1,64,32,64]{3,2,1,0:T(8,128)(2,1)S(1)} %get-tuple-element.15, bf16[1,64,32,64]{3,2,1,0:T(8,128)(2,1)S(1)} %get-tuple-element.14, ...), kind=kLoop, calls=%fused_computation.11 | loop fusion | flops 28148736 | bytes 12063744 | tf_op jit(solution)/shard_map/convert_element_type | solution.py:124
  118.4 1.2 fusion.14
  119.6 7.1 %subtract_multiply_fusion = f32[12,64,33,64]{3,2,1,0:T(8,128)} fusion(f32[14,66,34,64]{3,2,1,0:T(8,128)S(1)} %maximum_convert_fusion, f32[64,33,64]{2,1,0:T(8,128)S(1)} %get-tuple-element.13, f32[64,33,64]{2,1,0:T(8,128)S(1)} %get-tuple-element.12), kind=kLoop, calls=%fused_computation.4 | loop fusion | flops 9732096 | bytes 20545536 | tf_op jit(solution)/shard_map/mul | solution.py:36
  126.7 8.8 %subtract_multiply_fusion.1 = f32[12,65,32,64]{3,2,1,0:T(8,128)} fusion(f32[14,66,34,64]{3,2,1,0:T(8,128)S(1)} %maximum_convert_fusion, f32[65,32,64]{2,1,0:T(8,128)} %get-tuple-element.11, f32[65,32,64]{2,1,0:T(8,128)S(1)} %get-tuple-element.10), kind=kLoop, calls=%fused_computation.5 | loop fusion | flops 9584640 | bytes 20234240 | tf_op jit(solution)/shard_map/mul | solution.py:36
  135.5 27.3 %fusion.1 = f32[12,64,32,64]{3,2,1,0:T(8,128)} fusion(f32[12,64,32,64]{3,2,1,0:T(8,128)} %copy-done, f32[12,64,33,64]{3,2,1,0:T(8,128)} %subtract_multiply_fusion, f32[12,65,32,64]{3,2,1,0:T(8,128)} %subtract_multiply_fusion.1), kind=kLoop, calls=%fused_computation.8 | loop fusion | flops 7864320 | bytes 37748736 | tf_op jit(solution)/shard_map/sub | solution.py:139
  162.8 1.3 slice_multiply_fusion.1
  164.1 4.5 %multiply_reduce_fusion = f32[64,32,64]{2,1,0:T(8,128)S(1)} fusion(f32[12,64,32,64]{3,2,1,0:T(8,128)} %fusion.1, f32[8]{0:T(128)S(1)} %get-tuple-element.38), kind=kLoop, calls=%fused_computation.14 | loop fusion | flops 5111808 | bytes 4718624 | tf_op jit(solution)/shard_map/reduce_sum | solution.py:145
  169.1 0.7 gather_fusion.1
  170.0 4.4 %convolution_multiply_fusion.1 = f32[128,2,128]{2,1,0:T(2,128)S(1)} fusion(bf16[128,128,128]{2,1,0:T(8,128)(2,1)} %param.18, f32[128]{0:T(128)S(1)} %get-tuple-element.40, bf16[128,1,128]{2,1,0:T(2,128)(2,1)S(1)} %broadcast_select_fusion), kind=kOutput, calls=%fused_computation.21 | convolution fusion | flops 8421376 | bytes 4358656 | tf_op jit(solution)/shard_map/tec,tkc->tke/dot_general | solution.py:152
  174.9 1.5 collective-permute-start.23
  176.4 11.8 %reshape.133 = f32[12,64,2048]{2,1,0:T(8,128)} reshape(f32[12,64,32,64]{3,2,1,0:T(8,128)} %fusion.1) | data formatting | bytes 12582912 | tf_op jit(solution)/shard_map/reshape | solution.py:142
  188.1 5.5 %collective-permute-start.22 = (bf16[2,128]{1,0:T(2,128)(2,1)S(1)}, bf16[2,128]{1,0:T(2,128)(2,1)S(1)}, u32[]{:S(2)}, u32[]{:S(2)}) collective-permute-start(bf16[2,128]{1,0:T(2,128)(2,1)S(1)} %get-tuple-element.33), channel_id=1, source_target_pairs={{0,15},{1,0},{2,1},{3,2},{4,3},{5,4},{6,5},{7,6},{8,7},{9,8},{10,9... | collective-permute-start | bytes 1544 | tf_op jit(solution)/shard_map/ppermute | solution.py:18
  194.2 0.8 collective-permute-done.22
  194.9 5.6 %collective-permute-start.27 = (bf16[2,128]{1,0:T(2,128)(2,1)S(1)}, bf16[2,128]{1,0:T(2,128)(2,1)S(1)}, u32[]{:S(2)}, u32[]{:S(2)}) collective-permute-start(bf16[2,128]{1,0:T(2,128)(2,1)S(1)} %collective-permute-done.26), channel_id=1, source_target_pairs={{0,15},{1,0},{2,1},{3,2},{4,3},{5,4},{6,5},{7,6},{8,7},{9,8},{10,9... | collective-permute-start | bytes 1544 | tf_op jit(solution)/shard_map/ppermute | solution.py:18
  200.6 5.4 %collective-permute-start.20 = (bf16[2,128]{1,0:T(2,128)(2,1)S(1)}, bf16[2,128]{1,0:T(2,128)(2,1)S(1)}, u32[]{:S(2)}, u32[]{:S(2)}) collective-permute-start(bf16[2,128]{1,0:T(2,128)(2,1)S(1)} %collective-permute-done.19), channel_id=1, source_target_pairs={{0,15},{1,0},{2,1},{3,2},{4,3},{5,4},{6,5},{7,6},{8,7},{9,8},{10,9... | collective-permute-start | bytes 1544 | tf_op jit(solution)/shard_map/ppermute | solution.py:18
  206.0 1.4 collective-permute-done.24
  207.4 5.4 %collective-permute-done.17 = bf16[2,128]{1,0:T(2,128)(2,1)S(1)} collective-permute-done((bf16[2,128]{1,0:T(2,128)(2,1)S(1)}, bf16[2,128]{1,0:T(2,128)(2,1)S(1)}, u32[]{:S(2)}, u32[]{:S(2)}) %collective-permute-start.17) | collective-permute-done | bytes 544 | tf_op jit(solution)/shard_map/ppermute | solution.py:18
  (76 shorter events, 4.7 us)
Async XLA Ops:
  7.7 20.8 %collective-permute-start.10 = (bf16[2,12,128]{2,1,0:T(8,128)(2,1)S(1)}, bf16[2,12,128]{2,1,0:T(8,128)(2,1)S(1)}, u32[]{:S(2)}, u32[]{:S(2)}) collective-permute-start(bf16[2,12,128]{2,1,0:T(8,128)(2,1)S(1)} %get-tuple-element.21), channel_id=1, source_target_pairs={{0,16},{16,32},{32,48},{48,64},{64,80},{80,96},{96,112},{112,0},{1... | collective-permute-start | bytes 18440 | tf_op jit(solution)/shard_map/ppermute | solution.py:18
  7.7 28.9 %collective-permute-start.9 = (bf16[2,12,128]{2,1,0:T(8,128)(2,1)S(1)}, bf16[2,12,128]{2,1,0:T(8,128)(2,1)S(1)}, u32[]{:S(2)}, u32[]{:S(2)}) collective-permute-start(bf16[2,12,128]{2,1,0:T(8,128)(2,1)S(1)} %get-tuple-element.22), channel_id=1, source_target_pairs={{0,16},{16,32},{32,48},{48,64},{64,80},{80,96},{96,112},{112,0},{1... | collective-permute-start | bytes 18440 | tf_op jit(solution)/shard_map/ppermute | solution.py:18
  9.5 21.7 %collective-permute-start.7 = (bf16[2,12,128]{2,1,0:T(8,128)(2,1)S(1)}, bf16[2,12,128]{2,1,0:T(8,128)(2,1)S(1)}, u32[]{:S(2)}, u32[]{:S(2)}) collective-permute-start(bf16[2,12,128]{2,1,0:T(8,128)(2,1)S(1)} %get-tuple-element.23), channel_id=1, source_target_pairs={{0,16},{16,32},{32,48},{48,64},{64,80},{80,96},{96,112},{112,0},{1... | collective-permute-start | bytes 18440 | tf_op jit(solution)/shard_map/ppermute | solution.py:18
  9.5 21.7 %collective-permute-start.6 = (bf16[2,12,128]{2,1,0:T(8,128)(2,1)S(1)}, bf16[2,12,128]{2,1,0:T(8,128)(2,1)S(1)}, u32[]{:S(2)}, u32[]{:S(2)}) collective-permute-start(bf16[2,12,128]{2,1,0:T(8,128)(2,1)S(1)} %get-tuple-element.24), channel_id=1, source_target_pairs={{0,1},{1,2},{2,3},{3,4},{4,5},{5,6},{6,7},{7,8},{8,9},{9,10},{10,1... | collective-permute-start | bytes 18440 | tf_op jit(solution)/shard_map/ppermute | solution.py:18
  11.0 20.3 %collective-permute-start.5 = (bf16[2,12,128]{2,1,0:T(8,128)(2,1)S(1)}, bf16[2,12,128]{2,1,0:T(8,128)(2,1)S(1)}, u32[]{:S(2)}, u32[]{:S(2)}) collective-permute-start(bf16[2,12,128]{2,1,0:T(8,128)(2,1)S(1)} %get-tuple-element.26), channel_id=1, source_target_pairs={{0,15},{1,0},{2,1},{3,2},{4,3},{5,4},{6,5},{7,6},{8,7},{9,8},{10,9... | collective-permute-start | bytes 18440 | tf_op jit(solution)/shard_map/ppermute | solution.py:18
  17.2 30.8 %copy-start.2 = (s32[128]{0:T(128)S(1)}, s32[128]{0:T(128)}, u32[]{:S(2)}) copy-start(s32[128]{0:T(128)} %param.17) | copy-start | bytes 1540
  28.5 8.1 %collective-permute-start.3 = (bf16[2,12,128]{2,1,0:T(8,128)(2,1)S(1)}, bf16[2,12,128]{2,1,0:T(8,128)(2,1)S(1)}, u32[]{:S(2)}, u32[]{:S(2)}) collective-permute-start(bf16[2,12,128]{2,1,0:T(8,128)(2,1)S(1)} %get-tuple-element.27), channel_id=1, source_target_pairs={{0,112},{16,0},{32,16},{48,32},{64,48},{80,64},{96,80},{112,96},{1... | collective-permute-start | bytes 18440 | tf_op jit(solution)/shard_map/ppermute | solution.py:18
  31.2 5.6 %collective-permute-start = (bf16[2,12,128]{2,1,0:T(8,128)(2,1)S(1)}, bf16[2,12,128]{2,1,0:T(8,128)(2,1)S(1)}, u32[]{:S(2)}, u32[]{:S(2)}) collective-permute-start(bf16[2,12,128]{2,1,0:T(8,128)(2,1)S(1)} %get-tuple-element.20), channel_id=1, source_target_pairs={{0,112},{16,0},{32,16},{48,32},{64,48},{80,64},{96,80},{112,96},{1... | collective-permute-start | bytes 18440 | tf_op jit(solution)/shard_map/ppermute | solution.py:18
  31.2 10.9 %collective-permute-start.11 = (bf16[2,12,128]{2,1,0:T(8,128)(2,1)S(1)}, bf16[2,12,128]{2,1,0:T(8,128)(2,1)S(1)}, u32[]{:S(2)}, u32[]{:S(2)}) collective-permute-start(bf16[2,12,128]{2,1,0:T(8,128)(2,1)S(1)} %collective-permute-done.10), channel_id=1, source_target_pairs={{0,1},{1,2},{2,3},{3,4},{4,5},{5,6},{6,7},{7,8},{8,9},{9,10},{10,1... | collective-permute-start | bytes 18440 | tf_op jit(solution)/shard_map/ppermute | solution.py:18
  31.3 10.8 %collective-permute-start.8 = (bf16[2,12,128]{2,1,0:T(8,128)(2,1)S(1)}, bf16[2,12,128]{2,1,0:T(8,128)(2,1)S(1)}, u32[]{:S(2)}, u32[]{:S(2)}) collective-permute-start(bf16[2,12,128]{2,1,0:T(8,128)(2,1)S(1)} %collective-permute-done.7), channel_id=1, source_target_pairs={{0,15},{1,0},{2,1},{3,2},{4,3},{5,4},{6,5},{7,6},{8,7},{9,8},{10,9... | collective-permute-start | bytes 18440 | tf_op jit(solution)/shard_map/ppermute | solution.py:18
  36.6 5.5 %collective-permute-start.2 = (bf16[2,12,128]{2,1,0:T(8,128)(2,1)S(1)}, bf16[2,12,128]{2,1,0:T(8,128)(2,1)S(1)}, u32[]{:S(2)}, u32[]{:S(2)}) collective-permute-start(bf16[2,12,128]{2,1,0:T(8,128)(2,1)S(1)} %get-tuple-element.28), channel_id=1, source_target_pairs={{0,112},{16,0},{32,16},{48,32},{64,48},{80,64},{96,80},{112,96},{1... | collective-permute-start | bytes 18440 | tf_op jit(solution)/shard_map/ppermute | solution.py:18
  36.7 7.0 %collective-permute-start.4 = (bf16[2,12,128]{2,1,0:T(8,128)(2,1)S(1)}, bf16[2,12,128]{2,1,0:T(8,128)(2,1)S(1)}, u32[]{:S(2)}, u32[]{:S(2)}) collective-permute-start(bf16[2,12,128]{2,1,0:T(8,128)(2,1)S(1)} %collective-permute-done.3), channel_id=1, source_target_pairs={{0,1},{1,2},{2,3},{3,4},{4,5},{5,6},{6,7},{7,8},{8,9},{9,10},{10,1... | collective-permute-start | bytes 18440 | tf_op jit(solution)/shard_map/ppermute | solution.py:18
  36.8 7.0 %collective-permute-start.1 = (bf16[2,12,128]{2,1,0:T(8,128)(2,1)S(1)}, bf16[2,12,128]{2,1,0:T(8,128)(2,1)S(1)}, u32[]{:S(2)}, u32[]{:S(2)}) collective-permute-start(bf16[2,12,128]{2,1,0:T(8,128)(2,1)S(1)} %collective-permute-done), channel_id=1, source_target_pairs={{0,15},{1,0},{2,1},{3,2},{4,3},{5,4},{6,5},{7,6},{8,7},{9,8},{10,9... | collective-permute-start | bytes 18440 | tf_op jit(solution)/shard_map/ppermute | solution.py:18
  79.2 9.4 %copy-start = (f32[12,64,32,64]{3,2,1,0:T(8,128)}, f32[12,64,32,64]{3,2,1,0:T(8,128)S(1)}, u32[]{:S(2)}) copy-start(f32[12,64,32,64]{3,2,1,0:T(8,128)S(1)} %get-tuple-element.5) | copy-start | bytes 18874372
  79.2 9.4 %copy-start.1 = (bf16[12,64,32,64]{3,2,1,0:T(8,128)(2,1)}, bf16[12,64,32,64]{3,2,1,0:T(8,128)(2,1)S(1)}, u32[]{:S(2)}) copy-start(bf16[12,64,32,64]{3,2,1,0:T(8,128)(2,1)S(1)} %get-tuple-element.4) | copy-start | bytes 9437188
  80.9 4.4 %collective-permute-start.13 = (bf16[14,1,32,64]{3,2,1,0:T(8,128)(2,1)S(1)}, bf16[14,1,32,64]{3,2,1,0:T(8,128)(2,1)S(1)}, u32[]{:S(2)}, u32[]{:S(2)}) collective-permute-start(bf16[14,1,32,64]{3,2,1,0:T(8,128)(2,1)S(1)} %get-tuple-element.19), channel_id=1, source_target_pairs={{16,0},{32,16},{48,32},{64,48},{80,64},{96,80},{112,96},{17,1},{33... | collective-permute-start | bytes 172040 | tf_op jit(solution)/shard_map/ppermute | solution.py:29
  82.2 4.0 %collective-permute-start.12 = (bf16[14,1,32,64]{3,2,1,0:T(8,128)(2,1)S(1)}, bf16[14,1,32,64]{3,2,1,0:T(8,128)(2,1)S(1)}, u32[]{:S(2)}, u32[]{:S(2)}) collective-permute-start(bf16[14,1,32,64]{3,2,1,0:T(8,128)(2,1)S(1)} %get-tuple-element.18), channel_id=1, source_target_pairs={{0,16},{16,32},{32,48},{48,64},{64,80},{80,96},{96,112},{1,17},{17... | collective-permute-start | bytes 172040 | tf_op jit(solution)/shard_map/ppermute | solution.py:28
  88.5 14.7 %collective-permute-start.15 = (bf16[14,66,1,64]{3,2,1,0:T(2,128)(2,1)S(1)}, bf16[14,66,1,64]{3,2,1,0:T(2,128)(2,1)S(1)}, u32[]{:S(2)}, u32[]{:S(2)}) collective-permute-start(bf16[14,66,1,64]{3,2,1,0:T(2,128)(2,1)S(1)} %get-tuple-element.17), channel_id=1, source_target_pairs={{1,0},{2,1},{3,2},{4,3},{5,4},{6,5},{7,6},{8,7},{9,8},{10,9},{11,1... | collective-permute-start | bytes 354824 | tf_op jit(solution)/shard_map/ppermute | solution.py:29
  89.8 15.1 %collective-permute-start.14 = (bf16[14,66,1,64]{3,2,1,0:T(2,128)(2,1)S(1)}, bf16[14,66,1,64]{3,2,1,0:T(2,128)(2,1)S(1)}, u32[]{:S(2)}, u32[]{:S(2)}) collective-permute-start(bf16[14,66,1,64]{3,2,1,0:T(2,128)(2,1)S(1)} %get-tuple-element.16), channel_id=1, source_target_pairs={{0,1},{1,2},{2,3},{3,4},{4,5},{5,6},{6,7},{7,8},{8,9},{9,10},{10,1... | collective-permute-start | bytes 354824 | tf_op jit(solution)/shard_map/ppermute | solution.py:28
  174.8 18.8 %collective-permute-start.26 = (bf16[2,128]{1,0:T(2,128)(2,1)S(1)}, bf16[2,128]{1,0:T(2,128)(2,1)S(1)}, u32[]{:S(2)}, u32[]{:S(2)}) collective-permute-start(bf16[2,128]{1,0:T(2,128)(2,1)S(1)} %get-tuple-element.30), channel_id=1, source_target_pairs={{0,112},{16,0},{32,16},{48,32},{64,48},{80,64},{96,80},{112,96},{1... | collective-permute-start | bytes 1544 | tf_op jit(solution)/shard_map/ppermute | solution.py:18
  174.9 19.3 %collective-permute-start.23 = (bf16[2,128]{1,0:T(2,128)(2,1)S(1)}, bf16[2,128]{1,0:T(2,128)(2,1)S(1)}, u32[]{:S(2)}, u32[]{:S(2)}) collective-permute-start(bf16[2,128]{1,0:T(2,128)(2,1)S(1)} %get-tuple-element.32), channel_id=1, source_target_pairs={{0,112},{16,0},{32,16},{48,32},{64,48},{80,64},{96,80},{112,96},{1... | collective-permute-start | bytes 1544 | tf_op jit(solution)/shard_map/ppermute | solution.py:18
  188.1 6.8 %collective-permute-start.22 = (bf16[2,128]{1,0:T(2,128)(2,1)S(1)}, bf16[2,128]{1,0:T(2,128)(2,1)S(1)}, u32[]{:S(2)}, u32[]{:S(2)}) collective-permute-start(bf16[2,128]{1,0:T(2,128)(2,1)S(1)} %get-tuple-element.33), channel_id=1, source_target_pairs={{0,15},{1,0},{2,1},{3,2},{4,3},{5,4},{6,5},{7,6},{8,7},{9,8},{10,9... | collective-permute-start | bytes 1544 | tf_op jit(solution)/shard_map/ppermute | solution.py:18
  193.6 6.9 %collective-permute-start.21 = (bf16[2,128]{1,0:T(2,128)(2,1)S(1)}, bf16[2,128]{1,0:T(2,128)(2,1)S(1)}, u32[]{:S(2)}, u32[]{:S(2)}) collective-permute-start(bf16[2,128]{1,0:T(2,128)(2,1)S(1)} %get-tuple-element.35), channel_id=1, source_target_pairs={{0,1},{1,2},{2,3},{3,4},{4,5},{5,6},{6,7},{7,8},{8,9},{9,10},{10,1... | collective-permute-start | bytes 1544 | tf_op jit(solution)/shard_map/ppermute | solution.py:18
  193.6 6.9 %collective-permute-start.25 = (bf16[2,128]{1,0:T(2,128)(2,1)S(1)}, bf16[2,128]{1,0:T(2,128)(2,1)S(1)}, u32[]{:S(2)}, u32[]{:S(2)}) collective-permute-start(bf16[2,128]{1,0:T(2,128)(2,1)S(1)} %get-tuple-element.31), channel_id=1, source_target_pairs={{0,112},{16,0},{32,16},{48,32},{64,48},{80,64},{96,80},{112,96},{1... | collective-permute-start | bytes 1544 | tf_op jit(solution)/shard_map/ppermute | solution.py:18
  193.6 6.9 %collective-permute-start.19 = (bf16[2,128]{1,0:T(2,128)(2,1)S(1)}, bf16[2,128]{1,0:T(2,128)(2,1)S(1)}, u32[]{:S(2)}, u32[]{:S(2)}) collective-permute-start(bf16[2,128]{1,0:T(2,128)(2,1)S(1)} %get-tuple-element.36), channel_id=1, source_target_pairs={{0,16},{16,32},{32,48},{48,64},{64,80},{80,96},{96,112},{112,0},{1... | collective-permute-start | bytes 1544 | tf_op jit(solution)/shard_map/ppermute | solution.py:18
  194.1 11.8 %collective-permute-start.16 = (bf16[2,128]{1,0:T(2,128)(2,1)S(1)}, bf16[2,128]{1,0:T(2,128)(2,1)S(1)}, u32[]{:S(2)}, u32[]{:S(2)}) collective-permute-start(bf16[2,128]{1,0:T(2,128)(2,1)S(1)} %get-tuple-element.29), channel_id=1, source_target_pairs={{0,16},{16,32},{32,48},{48,64},{64,80},{80,96},{96,112},{112,0},{1... | collective-permute-start | bytes 1544 | tf_op jit(solution)/shard_map/ppermute | solution.py:18
  194.9 11.1 %collective-permute-start.27 = (bf16[2,128]{1,0:T(2,128)(2,1)S(1)}, bf16[2,128]{1,0:T(2,128)(2,1)S(1)}, u32[]{:S(2)}, u32[]{:S(2)}) collective-permute-start(bf16[2,128]{1,0:T(2,128)(2,1)S(1)} %collective-permute-done.26), channel_id=1, source_target_pairs={{0,15},{1,0},{2,1},{3,2},{4,3},{5,4},{6,5},{7,6},{8,7},{9,8},{10,9... | collective-permute-start | bytes 1544 | tf_op jit(solution)/shard_map/ppermute | solution.py:18
  200.5 6.9 %collective-permute-start.24 = (bf16[2,128]{1,0:T(2,128)(2,1)S(1)}, bf16[2,128]{1,0:T(2,128)(2,1)S(1)}, u32[]{:S(2)}, u32[]{:S(2)}) collective-permute-start(bf16[2,128]{1,0:T(2,128)(2,1)S(1)} %collective-permute-done.23), channel_id=1, source_target_pairs={{0,1},{1,2},{2,3},{3,4},{4,5},{5,6},{6,7},{7,8},{8,9},{9,10},{10,1... | collective-permute-start | bytes 1544 | tf_op jit(solution)/shard_map/ppermute | solution.py:18
  200.5 6.9 %collective-permute-start.18 = (bf16[2,128]{1,0:T(2,128)(2,1)S(1)}, bf16[2,128]{1,0:T(2,128)(2,1)S(1)}, u32[]{:S(2)}, u32[]{:S(2)}) collective-permute-start(bf16[2,128]{1,0:T(2,128)(2,1)S(1)} %get-tuple-element.37), channel_id=1, source_target_pairs={{0,16},{16,32},{32,48},{48,64},{64,80},{80,96},{96,112},{112,0},{1... | collective-permute-start | bytes 1544 | tf_op jit(solution)/shard_map/ppermute | solution.py:18
  200.6 6.8 %collective-permute-start.20 = (bf16[2,128]{1,0:T(2,128)(2,1)S(1)}, bf16[2,128]{1,0:T(2,128)(2,1)S(1)}, u32[]{:S(2)}, u32[]{:S(2)}) collective-permute-start(bf16[2,128]{1,0:T(2,128)(2,1)S(1)} %collective-permute-done.19), channel_id=1, source_target_pairs={{0,15},{1,0},{2,1},{3,2},{4,3},{5,4},{6,5},{7,6},{8,7},{9,8},{10,9... | collective-permute-start | bytes 1544 | tf_op jit(solution)/shard_map/ppermute | solution.py:18
  206.0 6.9 %collective-permute-start.17 = (bf16[2,128]{1,0:T(2,128)(2,1)S(1)}, bf16[2,128]{1,0:T(2,128)(2,1)S(1)}, u32[]{:S(2)}, u32[]{:S(2)}) collective-permute-start(bf16[2,128]{1,0:T(2,128)(2,1)S(1)} %collective-permute-done.16), channel_id=1, source_target_pairs={{0,1},{1,2},{2,3},{3,4},{4,5},{5,6},{6,7},{7,8},{8,9},{9,10},{10,1... | collective-permute-start | bytes 1544 | tf_op jit(solution)/shard_map/ppermute | solution.py:18
where the time goes:
time: 216 us; the launch traced here: 214 us
  other arithmetic  83.8 us (39%)
  starting transfers between devices  50.5 us (23%)
  local copies, waits for them, and re-layouts  44.9 us (21%)
  waiting for transfers between devices  20.5 us (9%)
  matrix products  12.7 us (6%)
    ppermute x24, starting transfers between devices, from_behind(): return lax.ppermute(value, axis, pairs)  40.1 us
    sub x1, other arithmetic, per_device(): state - time_step * (flux_x[:, 1:] - flux_x[:, :-1] + flux_y[:, :, 1:] -...  27.3 us
    mul x4, other arithmetic, face_flux(): return 0.5 * (speed * (q_lo + q_hi) - jnp.abs(speed) * (q_hi - q_lo))  17.3 us
    convert_element_type x1, other arithmetic, per_device(): with_halo(packed.astype(jnp.bfloat16), (('gx', 1), ('gy', 2)), 1)  13.2 us
    reshape x1, local copies, waits for them, and re-layouts, per_device(): remapped = fresh.reshape(count_q, width_x, width_y * NZ)  11.8 us
    reshape x1, local copies, waits for them, and re-layouts, per_device(): state = cell_state.reshape(count_q, width_x, width_y, NZ) + dep  11.4 us
    another operation x3, other arithmetic  10.8 us
    reshape x1, local copies, waits for them, and re-layouts, per_device(): dep = dep.reshape(count_q, width_x, width_y, NZ)  10.3 us
  transfers between devices with their start and end apart: 28, of which 7 were waited for; matrix products, arithmetic and copies ran while one was open for 11% of the time, Pallas kernels for 0%

commit v1 on v0

v1 whole, which is shorter than its diff:
```python
import functools

import jax
import jax.numpy as jnp
from jax import lax
from jax.experimental import pallas as pl
from jax.experimental.pallas import tpu as pltpu
from jax.sharding import PartitionSpec as P

MAT = 8
NQ = 12
NZ = 64
BLK = 128
CAP = 2
TIME_STEP = 0.8
NEAR = [(a, b) for a in range(3) for b in range(3)]
OWN = 4
F32 = jnp.float32
BF16 = jnp.bfloat16
MESH = pl.DeviceIdType.MESH


def kernel(
    dims,
    vol, vel, ene, mat, cell_v, dest_s, slot_s, cell_s, count_s, props_s, w_hbm, state_hbm,
    out_ref, eo_ref,
    wts, q_ref, f_ref, s_ref, c_ref, press, blk, outg, recv, xs, xr, ys, yr, anss, ret,
    w_sem, q_sem, o_sem, pay_s, pay_r, hx_s, hx_r, hy_s, hy_r, ret_s, ret_r,
):
    gx, gy, n_blk, n_tiles, wx, n_yb = dims
    px = lax.axis_index("gx")
    py = lax.axis_index("gy")
    group = 8
    n_chunk = 4
    tiles_chunk = n_tiles // n_chunk
    pad = 8
    row_x = pad + NQ * wx
    row_y = row_x + wx

    def dev(a, b, sign):
        return (lax.rem(px + sign * (a - 1) + gx, gx), lax.rem(py + sign * (b - 1) + gy, gy))

    def w_copy(i):
        part = pl.ds(i * tiles_chunk, tiles_chunk)
        return pltpu.make_async_copy(w_hbm.at[part], wts.at[part], w_sem.at[i])

    def q_copy(yb):
        return pltpu.make_async_copy(
            state_hbm.at[:, pl.ds(yb * BLK, BLK)],
            q_ref.at[yb + 1, pl.ds(pad, NQ * wx)],
            q_sem.at[yb],
        )

    def o_copy(yb):
        return pltpu.make_async_copy(
            f_ref.at[yb, pl.ds(0, NQ * wx)], out_ref.at[:, pl.ds(yb * BLK, BLK)], o_sem.at[yb]
        )

    ret[...] = jnp.zeros(ret.shape, F32)
    barrier = pltpu.get_barrier_semaphore()
    for a, b in NEAR:
        if (a, b) != (1, 1):
            pl.semaphore_signal(barrier, inc=1, device_id=dev(a, b, 1), device_id_type=MESH)
    for i in range(n_chunk):
        w_copy(i).start()
    for yb in range(n_yb):
        q_copy(yb).start()

    sub8 = lax.broadcasted_iota(jnp.int32, (8, BLK), 0)
    dens = [props_s[0, m] for m in range(MAT)]
    stiff = [props_s[1, m] for m in range(MAT)]
    dens_col = jnp.zeros((8, BLK), F32)
    for m in range(MAT):
        dens_col = jnp.where(sub8 == m, dens[m], dens_col)
    blk[...] = jnp.zeros(blk.shape, F32)
    for j in range(n_blk):
        hit = jnp.broadcast_to(mat[j : j + 1, :], (8, BLK)) == sub8
        v = vol[j : j + 1, :]
        blk[j, 0:8, :] = jnp.where(hit, jnp.broadcast_to(v, (8, BLK)), 0.0)
        mass = v * jnp.sum(jnp.where(hit, dens_col, 0.0), axis=0, keepdims=True)
        blk[j, 8:11, :] = mass * vel[:, j * BLK : (j + 1) * BLK]
        blk[j, 11:12, :] = mass * ene[j : j + 1, :]
    first, second = [], []
    keys = []
    for j in range(n_blk):
        d = dest_s[j]
        ka = lax.rem(d // gy - px + 1 + gx, gx)
        kb = lax.rem(lax.rem(d, gy) - py + 1 + gy, gy)
        keys.append(ka * 3 + kb)
    for n in range(9):
        low = jnp.int32(0)
        total = jnp.int32(0)
        for j in reversed(range(n_blk)):
            same = keys[j] == n
            low = jnp.where(same, jnp.int32(j), low)
            total = total + jnp.where(same, jnp.int32(j), jnp.int32(0))
        first.append(low)
        second.append(jnp.minimum(total - low, n_blk - 1))
    for n in range(9):
        for rank, src in ((0, first[n]), (1, second[n])):
            value = blk[src].astype(BF16)
            if n == OWN:
                recv[2 * n + rank] = value
            else:
                outg[2 * n + rank] = value

    pl.semaphore_wait(barrier, 8)
    pay = []
    for n, (a, b) in enumerate(NEAR):
        if n != OWN:
            i = len(pay)
            pay.append(
                pltpu.make_async_remote_copy(
                    src_ref=outg.at[pl.ds(2 * n, 2)], dst_ref=recv.at[pl.ds(2 * n, 2)],
                    send_sem=pay_s.at[i], recv_sem=pay_r.at[i],
                    device_id=dev(a, b, 1), device_id_type=MESH,
                )
            )
            pay[-1].start()

    rows_all = q_ref.shape[1]
    n_rows = 16 * wx

    def clear_end(i, carry):
        at = pl.multiple_of(i * 8, 8)
        q_ref[0, pl.ds(at, 8), :] = jnp.zeros((8, BLK), F32)
        q_ref[n_yb + 1, pl.ds(at, 8), :] = jnp.zeros((8, BLK), F32)
        return carry

    lax.fori_loop(0, rows_all // 8, clear_end, 0)

    def clear_tail(yb, carry):
        q_ref[yb + 1, 0:pad, :] = jnp.zeros((pad, BLK), F32)
        tail = rows_all - (row_y + wx)
        q_ref[yb + 1, row_y + wx : rows_all, :] = jnp.zeros((tail, BLK), F32)
        return carry

    lax.fori_loop(0, n_yb, clear_tail, 0)
    anss[...] = jnp.zeros(anss.shape, F32)

    for c in pay:
        c.wait_recv()
    for i in range(n_chunk):
        w_copy(i).wait()

    def local_slot(t):
        s = slot_s[t]
        source = s // CAP
        a = lax.rem(px - source // gy + 1 + gx, gx)
        b = lax.rem(py - lax.rem(source, gy) + 1 + gy, gy)
        return jnp.minimum((a * 3 + b) * CAP + lax.rem(s, CAP), n_blk - 1)

    def contrib(i, carry):
        for g in range(group):
            t = i * group + g
            c = jnp.dot(recv[local_slot(t)], wts[t], preferred_element_type=F32)
            s_ref[pl.ds(t, 16, stride=n_tiles), :] = c
        return carry

    lax.fori_loop(0, n_tiles // group, contrib, 0)

    def split(p, carry):
        for h in range(2):
            at = pl.multiple_of((2 * p + h) * n_tiles, n_tiles)
            value = s_ref[pl.ds(at, n_tiles), :]
            high = value.astype(BF16)
            c_ref[p, 0:n_tiles, h * BLK : (h + 1) * BLK] = high
            c_ref[p, n_tiles : 2 * n_tiles, h * BLK : (h + 1) * BLK] = (
                value - high.astype(F32)
            ).astype(BF16)
        return carry

    lax.fori_loop(0, NQ // 2, split, 0)

    lane_t = lax.broadcasted_iota(jnp.int32, (1, n_tiles), 1)
    cell_m = jnp.broadcast_to(jnp.where(lane_t < count_s[0], cell_v[...], -1), (wx, n_tiles))
    cell_at = lax.broadcasted_iota(jnp.int32, (wx, n_tiles), 0) * n_yb

    def deposit(yb):
        q_copy(yb).wait()
        pick = jnp.where(cell_m == cell_at + yb, 1.0, 0.0).astype(BF16)
        left = jnp.concatenate([pick, pick], axis=1)
        mass = jnp.ones((wx, BLK), F32)
        moving = []
        for p in range(NQ // 2):
            both = jnp.dot(left, c_ref[p], preferred_element_type=F32)
            for h in range(2):
                r = 2 * p + h
                rows = pl.ds(pad + r * wx, wx)
                value = q_ref[yb + 1, rows, :] + both[:, h * BLK : (h + 1) * BLK]
                q_ref[yb + 1, rows, :] = value
                if r < MAT:
                    mass = mass + dens[r] * value
                elif r < MAT + 2:
                    moving.append(value)
        q_ref[yb + 1, pl.ds(row_x, wx), :] = moving[0] / mass
        q_ref[yb + 1, pl.ds(row_y, wx), :] = moving[1] / mass

    def deposit_ends(i, carry):
        deposit(i * (n_yb - 1))
        return carry

    lax.fori_loop(0, 2, deposit_ends, 0)

    lane = lax.broadcasted_iota(jnp.int32, (wx, BLK), 1)
    upper = lane >= NZ

    def rows_of(r):
        return pl.ds(pad + r * wx, wx)

    def pair(yb, p, top):
        if p < NQ // 2:
            one, two = q_ref[yb + 1, rows_of(2 * p), :], q_ref[yb + 1, rows_of(2 * p + 1), :]
        else:
            one = q_ref[yb + 1, pl.ds(row_y, wx), :]
            two = one
        turned = pltpu.roll(one, NZ, axis=1)
        return jnp.where(upper, two, turned) if top else jnp.where(upper, turned, two)

    for p in range(NQ // 2 + 1):
        ys[0, p] = pair(0, p, False).astype(BF16)
        ys[1, p] = pair(n_yb - 1, p, True).astype(BF16)
    halo = []
    for e, b in ((0, 0), (1, 2)):
        halo.append(
            pltpu.make_async_remote_copy(
                src_ref=ys.at[e], dst_ref=yr.at[1 - e], send_sem=hy_s.at[e], recv_sem=hy_r.at[1 - e],
                device_id=dev(1, b, 1), device_id_type=MESH,
            )
        )
        halo[-1].start()

    def deposit_inner(i, carry):
        deposit(i)
        return carry

    lax.fori_loop(1, n_yb - 1, deposit_inner, 0)

    def pack_x(yb, carry):
        xs[0, yb] = q_ref[yb + 1, pl.ds(pad, 16, stride=wx), :].astype(BF16)
        xs[1, yb] = q_ref[yb + 1, pl.ds(pad + wx - 1, 16, stride=wx), :].astype(BF16)
        return carry

    lax.fori_loop(0, n_yb, pack_x, 0)
    for e, a in ((0, 0), (1, 2)):
        halo.append(
            pltpu.make_async_remote_copy(
                src_ref=xs.at[e], dst_ref=xr.at[1 - e], send_sem=hx_s.at[e], recv_sem=hx_r.at[1 - e],
                device_id=dev(a, 1, 1), device_id_type=MESH,
            )
        )
        halo[-1].start()

    half = wx // 2
    sub = lax.broadcasted_iota(jnp.int32, (half, BLK), 0)
    lane_h = lax.broadcasted_iota(jnp.int32, (half, BLK), 1)
    upper_h = lane_h >= NZ

    def remap(yb, carry):
        for part in range(2):
            x0 = part * half

            def at(base, shift=0):
                return pl.ds(base + x0 + shift, half)

            ux = q_ref[yb + 1, at(row_x), :]
            lo = 0.5 * (q_ref[yb + 1, at(row_x, -1), :] + ux)
            hi = 0.5 * (ux + q_ref[yb + 1, at(row_x, 1), :])
            if part == 0:
                lo = jnp.where(sub == 0, 0.0, lo)
            else:
                hi = jnp.where(sub == half - 1, 0.0, hi)
            uy = q_ref[yb + 1, at(row_y), :]
            prev, after = q_ref[yb, at(row_y), :], q_ref[yb + 2, at(row_y), :]
            y_hi = 0.5 * (uy + pltpu.roll(jnp.where(upper_h, uy, after), NZ, axis=1))
            y_lo = 0.5 * (uy + pltpu.roll(jnp.where(upper_h, prev, uy), NZ, axis=1))
            place = lane_h + yb * BLK
            y_lo = jnp.where(place < NZ, 0.0, y_lo)
            y_hi = jnp.where(place >= n_yb * BLK - NZ, 0.0, y_hi)
            c_xm = TIME_STEP * jnp.maximum(lo, 0.0)
            c_xp = -TIME_STEP * jnp.minimum(hi, 0.0)
            c_ym = TIME_STEP * jnp.maximum(y_lo, 0.0)
            c_yp = -TIME_STEP * jnp.minimum(y_hi, 0.0)
            c_0 = 1.0 - TIME_STEP * (
                (jnp.maximum(hi, 0.0) - jnp.minimum(lo, 0.0))
                + (jnp.maximum(y_hi, 0.0) - jnp.minimum(y_lo, 0.0))
            )
            t_p = pltpu.roll(c_yp, NZ, axis=1)
            t_m = pltpu.roll(c_ym, NZ, axis=1)
            own = jnp.where(upper_h, t_p, t_m)
            other = jnp.where(upper_h, t_m, t_p)
            acc = jnp.zeros((half, BLK), F32)
            for r in range(NQ):
                base = pad + r * wx
                q = q_ref[yb + 1, at(base), :]
                beside = jnp.where(upper_h, q_ref[yb, at(base), :], q_ref[yb + 2, at(base), :])
                fresh = (
                    c_0 * q
                    + c_xm * q_ref[yb + 1, at(base, -1), :]
                    + c_xp * q_ref[yb + 1, at(base, 1), :]
                    + pltpu.roll(own * q + other * beside, NZ, axis=1)
                )
                f_ref[yb, pl.ds(r * wx + x0, half), :] = fresh
                if r < MAT:
                    acc = acc + fresh * (stiff[r] + (0.5 * stiff[r]) * fresh)
                elif r == NQ - 1:
                    acc = acc + 0.4 * fresh
            press[pl.ds(pl.multiple_of(yb * wx + x0, half), half), :] = acc.astype(BF16).astype(F32)
        return carry

    lax.fori_loop(0, n_yb, remap, 0)

    for c in halo[:2]:
        c.wait_recv()
    has = [
        jnp.where(py > 0, 1.0, 0.0).astype(F32),
        jnp.where(py < gy - 1, 1.0, 0.0).astype(F32),
    ]
    for e, yb in ((0, 0), (1, n_yb - 1)):
        inside = jnp.logical_not(upper) if e == 0 else upper
        speed = 0.5 * (q_ref[yb + 1, pl.ds(row_y, wx), :] + has[e] * yr[e, NQ // 2].astype(F32))
        speed = jnp.where(inside, TIME_STEP * speed, 0.0)
        pos, neg = jnp.maximum(speed, 0.0), jnp.minimum(speed, 0.0)
        w_far, w_own = (has[e] * pos, neg) if e == 0 else (-has[e] * neg, -pos)
        acc = jnp.zeros((wx, BLK), F32)
        for p in range(NQ // 2):
            packed = yr[e, p].astype(F32)
            for h in range(2):
                r = 2 * p + h
                far = packed if h == 0 else pltpu.roll(packed, NZ, axis=1)
                rows = pl.ds(r * wx, wx)
                fresh = f_ref[yb, rows, :] + (w_far * far + w_own * q_ref[yb + 1, rows_of(r), :])
                f_ref[yb, rows, :] = fresh
                if r < MAT:
                    acc = acc + fresh * (stiff[r] + (0.5 * stiff[r]) * fresh)
                elif r == NQ - 1:
                    acc = acc + 0.4 * fresh
        press[yb * wx : (yb + 1) * wx, :] = acc.astype(BF16).astype(F32)

    for c in halo[2:]:
        c.wait_recv()
    sub16 = lax.broadcasted_iota(jnp.int32, (16, BLK), 0)
    lin = jnp.zeros((16, BLK), F32)
    for m in range(MAT):
        lin = jnp.where(sub16 == m, stiff[m], lin)
    quad = 0.5 * lin
    lin = jnp.where(sub16 == NQ - 1, 0.4, lin)
    has = [
        jnp.where(px > 0, 1.0, 0.0).astype(F32),
        jnp.where(px < gx - 1, 1.0, 0.0).astype(F32),
    ]

    def border_x(yb, carry):
        for e, x in ((0, 0), (1, wx - 1)):
            far = xr[e, yb].astype(F32) * has[e]
            q = q_ref[yb + 1, pl.ds(pad + x, 16, stride=wx), :]
            speed = (0.5 * TIME_STEP) * (q[NQ : NQ + 1] + far[NQ : NQ + 1])
            pos, neg = jnp.maximum(speed, 0.0), jnp.minimum(speed, 0.0)
            change = (pos * far + neg * q) if e == 0 else -(pos * q + neg * far)
            rows = pl.ds(x, 16, stride=wx)
            fresh = f_ref[yb, rows, :] + change
            f_ref[yb, rows, :] = fresh
            terms = jnp.where(sub16 < NQ, fresh * (lin + quad * fresh), 0.0)
            value = jnp.sum(terms, axis=0, keepdims=True)
            press[pl.ds(yb * wx + x, 1), :] = value.astype(BF16).astype(F32)
        o_copy(yb).start()
        return carry

    lax.fori_loop(0, n_yb, border_x, 0)

    sub48 = lax.broadcasted_iota(jnp.int32, (48, BLK), 0)
    count = count_s[0]

    def sample(i, acc):
        lefts, rights = [], []
        for g in range(group):
            t = i * group + g
            s = jnp.where(t < count, local_slot(t), jnp.int32(100))
            c = cell_s[t]
            row = lax.rem(c, n_yb) * wx + c // n_yb
            value = press[pl.ds(row, 1), :]
            value = jnp.where(sub48 == s, jnp.broadcast_to(value, (48, BLK)), 0.0)
            lefts.append(jnp.where(sub48 == s + 24, 1.0, value).astype(BF16))
            rights.append(wts[t])
        return acc + lax.dot_general(
            jnp.concatenate(lefts, axis=1), jnp.concatenate(rights, axis=1),
            (((1,), (1,)), ((), ())), preferred_element_type=F32,
        )

    acc = lax.fori_loop(0, n_tiles // group, sample, jnp.zeros((48, BLK), F32))
    answer = (acc[0:24] / jnp.maximum(acc[24:48], 1.0)).astype(BF16).astype(F32)

    back = []
    for n, (a, b) in enumerate(NEAR):
        rows = slice(8 * n, 8 * n + 2)
        if n == OWN:
            ret[rows, :] = answer[2 * n : 2 * n + 2]
        else:
            anss[rows, :] = answer[2 * n : 2 * n + 2]
    for n, (a, b) in enumerate(NEAR):
        if n != OWN:
            i = len(back)
            back.append(
                pltpu.make_async_remote_copy(
                    src_ref=anss.at[pl.ds(8 * n, 8)], dst_ref=ret.at[pl.ds(8 * n, 8)],
                    send_sem=ret_s.at[i], recv_sem=ret_r.at[i],
                    device_id=dev(a, b, -1), device_id_type=MESH,
                )
            )
            back[-1].start()
    sub32 = lax.broadcasted_iota(jnp.int32, (32, BLK), 0)
    lane32 = lax.broadcasted_iota(jnp.int32, (32, BLK), 1)
    wanted = jnp.full((32, BLK), -1, jnp.int32)
    for n in range(9):
        wanted = jnp.where(sub32 == first[n], 8 * n, wanted)
        wanted = jnp.where(sub32 == second[n], 8 * n + 1, wanted)
    mine = jnp.where(wanted == lane32, 1.0, 0.0).astype(BF16)
    for c in pay + halo:
        c.wait_send()
    for c in back:
        c.wait_recv()
    result = jnp.dot(mine, ret[...].astype(BF16), preferred_element_type=F32)
    eo_ref[...] = result[0:n_blk]
    for yb in range(n_yb):
        o_copy(yb).wait()
    for c in back:
        c.wait_send()


def per_device(
    elem_volume, elem_velocity, elem_energy, elem_mat, elem_dest, tile_slot, tile_cell,
    tile_weight, tile_count, cell_state, mat_props,
):
    gx, gy = lax.axis_size("gx"), lax.axis_size("gy")
    n_blk = elem_dest.shape[0]
    n_tiles = tile_weight.shape[0]
    wx, lanes = cell_state.shape[1], cell_state.shape[2]
    n_yb = lanes // BLK
    rows_q = 16 * wx + 16
    vmem = pl.BlockSpec(memory_space=pltpu.VMEM)
    smem = pl.BlockSpec(memory_space=pltpu.SMEM)
    hbm = pl.BlockSpec(memory_space=pl.ANY)
    dma = pltpu.SemaphoreType.DMA
    out, eo = pl.pallas_call(
        functools.partial(kernel, (gx, gy, n_blk, n_tiles, wx, n_yb)),
        out_shape=(
            jax.ShapeDtypeStruct((NQ * wx, lanes), F32),
            jax.ShapeDtypeStruct((n_blk, BLK), F32),
        ),
        in_specs=[vmem] * 5 + [smem] * 5 + [hbm] * 2,
        out_specs=(hbm, vmem),
        scratch_shapes=[
            pltpu.VMEM((n_tiles, BLK, BLK), BF16),
            pltpu.VMEM((n_yb + 2, rows_q, BLK), F32),
            pltpu.VMEM((n_yb, 16 * wx, BLK), F32),
            pltpu.VMEM((16 * n_tiles, BLK), F32),
            pltpu.VMEM((NQ // 2, 2 * n_tiles, 2 * BLK), BF16),
            pltpu.VMEM((n_yb * wx, BLK), F32),
            pltpu.VMEM((n_blk, 16, BLK), F32),
            pltpu.VMEM((n_blk, 16, BLK), BF16),
            pltpu.VMEM((n_blk, 16, BLK), BF16),
            pltpu.VMEM((2, n_yb, 16, BLK), BF16),
            pltpu.VMEM((2, n_yb, 16, BLK), BF16),
            pltpu.VMEM((2, NQ // 2 + 1, wx, BLK), BF16),
            pltpu.VMEM((2, NQ // 2 + 1, wx, BLK), BF16),
            pltpu.VMEM((128, BLK), F32),
            pltpu.VMEM((128, BLK), F32),
            dma((4,)), dma((n_yb,)), dma((n_yb,)),
            dma((8,)), dma((8,)), dma((2,)), dma((2,)), dma((2,)), dma((2,)), dma((8,)), dma((8,)),
        ],
        compiler_params=pltpu.CompilerParams(
            collective_id=0, has_side_effects=True, vmem_limit_bytes=56 * 1024 * 1024
        ),
    )(
        elem_volume.reshape(n_blk, BLK), elem_velocity, elem_energy.reshape(n_blk, BLK),
        elem_mat.reshape(n_blk, BLK), tile_cell.reshape(1, n_tiles),
        elem_dest, tile_slot, tile_cell, tile_count, mat_props,
        tile_weight, cell_state.reshape(NQ * wx, lanes),
    )
    return out.reshape(NQ, wx, lanes), eo.astype(BF16).reshape(n_blk * BLK)


def solution(mesh):
    both = ("gx", "gy")
    return jax.shard_map(
        per_device,
        mesh=mesh,
        in_specs=(
            P(both), P(None, both), P(both), P(both), P(both), P(both), P(both),
            P(both, None, None), P(both), P(None, "gx", "gy"), P(),
        ),
        out_specs=(P(None, "gx", "gy"), P(both)),
        check_vma=False,
    )
```

time: 216 us -> 49.9 us (0.23)
  other arithmetic: 83.8 us -> 1.3 us
  starting transfers between devices: 50.5 us -> 0 us
  Pallas kernels: 0 us -> 40.7 us
  local copies, waits for them, and re-layouts: 44.9 us -> 6.28 us
  waiting for transfers between devices: 20.5 us -> 0 us
  matrix products: 12.7 us -> 0 us
    ppermute x28 -> x0, starting transfers between devices: 50.5 us -> none  [the longest x24 40.1 us: from_behind(): return lax.ppermute(value, axis, pairs)]
    pallas_call x0 -> x1, Pallas kernels: none -> 40.7 us  [per_device(): pl.pallas_call(functools.partial(kernel, (gx, gy, n_blk, n_tiles, wx, n_y...]
    reshape x4 -> x0, local copies, waits for them, and re-layouts: 33.4 us -> none  [the longest x1 11.8 us: per_device(): remapped = fresh.reshape(count_q, width_x, width_y * NZ)]
    sub x1 -> x0, other arithmetic: 27.3 us -> none  [per_device(): state - time_step * (flux_x[:, 1:] - flux_x[:, :-1] + flux_y[:, :, 1:] -...]
    ppermute x28 -> x0, waiting for transfers between devices: 20.5 us -> none  [the longest x24 9.26 us: from_behind(): return lax.ppermute(value, axis, pairs)]
    mul x5 -> x0, other arithmetic: 18.6 us -> none  [the longest x4 17.3 us: face_flux(): return 0.5 * (speed * (q_lo + q_hi) - jnp.abs(speed) * (q_hi - q_lo))]
    convert_element_type x3 -> x0, other arithmetic: 13.2 us -> none  [the longest x1 13.2 us: per_device(): with_halo(packed.astype(jnp.bfloat16), (('gx', 1), ('gy', 2)), 1)]
    dot_general x4 -> x0, matrix products: 12.7 us -> none  [the longest x1 4.64 us: per_device(): jnp.einsum('kt,rtc->rkc', cell_pick, contrib, precision=lax.Precision.HIG...]
  transfers between devices with their start and end apart: 28 -> 0, of which waited for: 7 -> 0; matrix products, arithmetic and copies ran while one was open for 11% -> 0% of each run, Pallas kernels for 0% -> 0%
where the time goes in v1:
time: 49.9 us; the launch traced here: 49.6 us
  Pallas kernels  40.7 us (82%)
  local copies, waits for them, and re-layouts  6.28 us (13%)
  other arithmetic  1.3 us (3%)
  between operations  1.29 us (3%)
    pallas_call x1, Pallas kernels, per_device(): pl.pallas_call(functools.partial(kernel, (gx, gy, n_blk, n_tiles, wx, n_y...  40.7 us
    unnamed x1, local copies, waits for them, and re-layouts  6.28 us
    reshape x1, other arithmetic, per_device(): return (out.reshape(NQ, wx, lanes), eo.astype(BF16).reshape(n_blk * BLK))  1.3 us

profile of v1, /device:TPU:0, one launch (start us, length us, event | category | flops | bytes accessed | tf_op | source)
XLA Modules:
  0.0 49.6 jit_solution(420139681755352689)
XLA Ops:
  1.3 40.7 %shard_map.122 = (f32[768,2048]{1,0:T(8,128)}, f32[18,128]{1,0:T(8,128)}) custom-call(f32[18,128]{1,0:T(8,128)} %bitcast.10, f32[3,2304]{1,0:T(4,128)} %vel.1, f32[18,128]{1,0:T(8,128)} %bitcast.11, s32[18,128]{1,0:T(8,128)} %bitcast.12, s32[1,128]{1,0:T(1,128)} %bitcast.13, s32[18]{0:T(128)} %dest_s.1, s32[128]{0:T(128)} %slot_s.1, s32[128]{0:T(128)} %cell_s.1, ...), custom_call_target="tpu_custom_call" | custom-call | tf_op jit(solution)/shard_map/pallas_call | solution.py:444
  42.0 1.3 %convert_bitcast_fusion = bf16[2304]{0:T(1024)(128)(2,1)} fusion(f32[18,128]{1,0:T(8,128)} %get-tuple-element.5), kind=kLoop, calls=%fused_computation | loop fusion | flops 2304 | bytes 13824 | tf_op jit(solution)/shard_map/reshape | solution.py:480
  43.3 6.3 %copy.15 = f32[12,64,2048]{2,1,0:T(8,128)} copy(f32[12,64,2048]{2,1,0:T(8,128)} %bitcast.8) | data formatting | bytes 12582912

commit v2 on v1

--- a/solution.py
+++ b/solution.py
@@ -23,14 +23,17 @@
 def kernel(
     dims,
     vol, vel, ene, mat, cell_v, dest_s, slot_s, cell_s, count_s, props_s, w_hbm, state_hbm,
-    out_ref, eo_ref,
-    wts, q_ref, f_ref, s_ref, c_ref, press, blk, outg, recv, xs, xr, ys, yr, anss, ret,
-    w_sem, q_sem, o_sem, pay_s, pay_r, hx_s, hx_r, hy_s, hy_r, ret_s, ret_r,
+    f_ref, eo_ref,
+    wts, q_ref, xe, fe, loc_s, row_s, s_ref, c_ref, press, blk, outg, recv, xs, xr, ys, yr, anss, ret,
+    w_sem, q_sem, pay_s, pay_r, hx_s, hx_r, hy_s, hy_r, ret_s, ret_r,
 ):
     gx, gy, n_blk, n_tiles, wx, n_yb = dims
     px = lax.axis_index("gx")
     py = lax.axis_index("gy")
-    group = 8
+    group = 16
+    pitch = n_tiles + 1
+    bits_y, bits_b, bits_x = gy.bit_length() - 1, n_yb.bit_length() - 1, wx.bit_length() - 1
+    assert (gx & (gx - 1), gy, n_yb, wx, CAP) == (0, 1 << bits_y, 1 << bits_b, 1 << bits_x, 2)
     n_chunk = 4
     tiles_chunk = n_tiles // n_chunk
     pad = 8
@@ -49,11 +52,6 @@
             state_hbm.at[:, pl.ds(yb * BLK, BLK)],
             q_ref.at[yb + 1, pl.ds(pad, NQ * wx)],
             q_sem.at[yb],
-        )
-
-    def o_copy(yb):
-        return pltpu.make_async_copy(
-            f_ref.at[yb, pl.ds(0, NQ * wx)], out_ref.at[:, pl.ds(yb * BLK, BLK)], o_sem.at[yb]
         )
 
     ret[...] = jnp.zeros(ret.shape, F32)
@@ -63,8 +61,6 @@
             pl.semaphore_signal(barrier, inc=1, device_id=dev(a, b, 1), device_id_type=MESH)
     for i in range(n_chunk):
         w_copy(i).start()
-    for yb in range(n_yb):
-        q_copy(yb).start()
 
     sub8 = lax.broadcasted_iota(jnp.int32, (8, BLK), 0)
     dens = [props_s[0, m] for m in range(MAT)]
@@ -84,8 +80,8 @@
     keys = []
     for j in range(n_blk):
         d = dest_s[j]
-        ka = lax.rem(d // gy - px + 1 + gx, gx)
-        kb = lax.rem(lax.rem(d, gy) - py + 1 + gy, gy)
+        ka = ((d >> bits_y) - px + 1) & (gx - 1)
+        kb = (d - py + 1) & (gy - 1)
         keys.append(ka * 3 + kb)
     for n in range(9):
         low = jnp.int32(0)
@@ -118,6 +114,12 @@
             )
             pay[-1].start()
 
+    def load_state(yb, carry):
+        q_copy(yb).start()
+        return carry
+
+    lax.fori_loop(0, n_yb, load_state, 0)
+
     rows_all = q_ref.shape[1]
     n_rows = 16 * wx
 
@@ -138,69 +140,91 @@
     lax.fori_loop(0, n_yb, clear_tail, 0)
     anss[...] = jnp.zeros(anss.shape, F32)
 
+    def clear_edge(yb, carry):
+        for e in range(2):
+            xe[e, yb] = jnp.zeros((16, BLK), F32)
+            fe[e, yb] = jnp.zeros((16, BLK), F32)
+        return carry
+
+    lax.fori_loop(0, n_yb, clear_edge, 0)
+
     for c in pay:
         c.wait_recv()
     for i in range(n_chunk):
         w_copy(i).wait()
 
+    count = count_s[0]
+
     def local_slot(t):
         s = slot_s[t]
-        source = s // CAP
-        a = lax.rem(px - source // gy + 1 + gx, gx)
-        b = lax.rem(py - lax.rem(source, gy) + 1 + gy, gy)
-        return jnp.minimum((a * 3 + b) * CAP + lax.rem(s, CAP), n_blk - 1)
+        a = (px + 1 - (s >> (bits_y + 1))) & (gx - 1)
+        b = (py + 1 - (s >> 1)) & (gy - 1)
+        return jnp.minimum(a * 6 + b * 2 + (s & 1), n_blk - 1)
 
     def contrib(i, carry):
         for g in range(group):
             t = i * group + g
-            c = jnp.dot(recv[local_slot(t)], wts[t], preferred_element_type=F32)
-            s_ref[pl.ds(t, 16, stride=n_tiles), :] = c
+            at = local_slot(t)
+            loc_s[t] = jnp.where(t < count, at, jnp.int32(100))
+            cell = cell_s[t]
+            row_s[t] = ((cell & (n_yb - 1)) << bits_x) + (cell >> bits_b)
+            c = jnp.dot(recv[at], wts[t], preferred_element_type=F32)
+            s_ref[pl.ds(t, 16, stride=pitch), :] = c
         return carry
 
     lax.fori_loop(0, n_tiles // group, contrib, 0)
 
-    def split(p, carry):
+    for p in range(NQ // 2):
         for h in range(2):
-            at = pl.multiple_of((2 * p + h) * n_tiles, n_tiles)
-            value = s_ref[pl.ds(at, n_tiles), :]
+            value = s_ref[pl.ds((2 * p + h) * pitch, n_tiles), :]
             high = value.astype(BF16)
             c_ref[p, 0:n_tiles, h * BLK : (h + 1) * BLK] = high
             c_ref[p, n_tiles : 2 * n_tiles, h * BLK : (h + 1) * BLK] = (
                 value - high.astype(F32)
             ).astype(BF16)
-        return carry
-
-    lax.fori_loop(0, NQ // 2, split, 0)
 
     lane_t = lax.broadcasted_iota(jnp.int32, (1, n_tiles), 1)
-    cell_m = jnp.broadcast_to(jnp.where(lane_t < count_s[0], cell_v[...], -1), (wx, n_tiles))
+    cell_m = jnp.broadcast_to(jnp.where(lane_t < count, cell_v[...], -1), (wx, n_tiles))
     cell_at = lax.broadcasted_iota(jnp.int32, (wx, n_tiles), 0) * n_yb
 
-    def deposit(yb):
-        q_copy(yb).wait()
-        pick = jnp.where(cell_m == cell_at + yb, 1.0, 0.0).astype(BF16)
-        left = jnp.concatenate([pick, pick], axis=1)
-        mass = jnp.ones((wx, BLK), F32)
-        moving = []
+    def deposit(one, two):
+        picks = []
+        for yb in (one, two):
+            q_copy(yb).wait()
+            picks.append(jnp.where(cell_m == cell_at + yb, 1.0, 0.0).astype(BF16))
+        left = jnp.concatenate(
+            [jnp.concatenate([pick, pick], axis=1) for pick in picks], axis=0
+        )
+        mass = [jnp.ones((wx, BLK), F32) for _ in range(2)]
+        moving = [[], []]
         for p in range(NQ // 2):
             both = jnp.dot(left, c_ref[p], preferred_element_type=F32)
-            for h in range(2):
-                r = 2 * p + h
-                rows = pl.ds(pad + r * wx, wx)
-                value = q_ref[yb + 1, rows, :] + both[:, h * BLK : (h + 1) * BLK]
-                q_ref[yb + 1, rows, :] = value
-                if r < MAT:
-                    mass = mass + dens[r] * value
-                elif r < MAT + 2:
-                    moving.append(value)
-        q_ref[yb + 1, pl.ds(row_x, wx), :] = moving[0] / mass
-        q_ref[yb + 1, pl.ds(row_y, wx), :] = moving[1] / mass
-
-    def deposit_ends(i, carry):
-        deposit(i * (n_yb - 1))
-        return carry
-
-    lax.fori_loop(0, 2, deposit_ends, 0)
+            for k, yb in enumerate((one, two)):
+                for h in range(2):
+                    r = 2 * p + h
+                    rows = pl.ds(pad + r * wx, wx)
+                    value = (
+                        q_ref[yb + 1, rows, :]
+                        + both[k * wx : (k + 1) * wx, h * BLK : (h + 1) * BLK]
+                    )
+                    q_ref[yb + 1, rows, :] = value
+                    xe[0, yb, r : r + 1, :] = value[0:1]
+                    xe[1, yb, r : r + 1, :] = value[wx - 1 : wx]
+                    if r < MAT:
+                        mass[k] = mass[k] + dens[r] * value
+                    elif r < MAT + 2:
+                        moving[k].append(value)
+        for k, yb in enumerate((one, two)):
+            scale = (0.5 * TIME_STEP) / mass[k]
+            u = moving[k][0] * scale
+            q_ref[yb + 1, pl.ds(row_x, wx), :] = u
+            q_ref[yb + 1, pl.ds(row_y, wx), :] = moving[k][1] * scale
+            xe[0, yb, NQ : NQ + 1, :] = u[0:1]
+            xe[1, yb, NQ : NQ + 1, :] = u[wx - 1 : wx]
+            for e in range(2):
+                xs[e, yb] = xe[e, yb].astype(BF16)
+
+    deposit(0, n_yb - 1)
 
     lane = lax.broadcasted_iota(jnp.int32, (wx, BLK), 1)
     upper = lane >= NZ
@@ -231,17 +255,11 @@
         halo[-1].start()
 
     def deposit_inner(i, carry):
-        deposit(i)
-        return carry
-
-    lax.fori_loop(1, n_yb - 1, deposit_inner, 0)
-
-    def pack_x(yb, carry):
-        xs[0, yb] = q_ref[yb + 1, pl.ds(pad, 16, stride=wx), :].astype(BF16)
-        xs[1, yb] = q_ref[yb + 1, pl.ds(pad + wx - 1, 16, stride=wx), :].astype(BF16)
-        return carry
-
-    lax.fori_loop(0, n_yb, pack_x, 0)
+        deposit(2 * i + 1, 2 * i + 2)
+        return carry
+
+    lax.fori_loop(0, n_yb // 2 - 1, deposit_inner, 0)
+
     for e, a in ((0, 0), (1, 2)):
         halo.append(
             pltpu.make_async_remote_copy(
@@ -264,26 +282,25 @@
                 return pl.ds(base + x0 + shift, half)
 
             ux = q_ref[yb + 1, at(row_x), :]
-            lo = 0.5 * (q_ref[yb + 1, at(row_x, -1), :] + ux)
-            hi = 0.5 * (ux + q_ref[yb + 1, at(row_x, 1), :])
+            lo = q_ref[yb + 1, at(row_x, -1), :] + ux
+            hi = ux + q_ref[yb + 1, at(row_x, 1), :]
             if part == 0:
                 lo = jnp.where(sub == 0, 0.0, lo)
             else:
                 hi = jnp.where(sub == half - 1, 0.0, hi)
             uy = q_ref[yb + 1, at(row_y), :]
             prev, after = q_ref[yb, at(row_y), :], q_ref[yb + 2, at(row_y), :]
-            y_hi = 0.5 * (uy + pltpu.roll(jnp.where(upper_h, uy, after), NZ, axis=1))
-            y_lo = 0.5 * (uy + pltpu.roll(jnp.where(upper_h, prev, uy), NZ, axis=1))
+            y_hi = uy + pltpu.roll(jnp.where(upper_h, uy, after), NZ, axis=1)
+            y_lo = uy + pltpu.roll(jnp.where(upper_h, prev, uy), NZ, axis=1)
             place = lane_h + yb * BLK
             y_lo = jnp.where(place < NZ, 0.0, y_lo)
             y_hi = jnp.where(place >= n_yb * BLK - NZ, 0.0, y_hi)
-            c_xm = TIME_STEP * jnp.maximum(lo, 0.0)
-            c_xp = -TIME_STEP * jnp.minimum(hi, 0.0)
-            c_ym = TIME_STEP * jnp.maximum(y_lo, 0.0)
-            c_yp = -TIME_STEP * jnp.minimum(y_hi, 0.0)
-            c_0 = 1.0 - TIME_STEP * (
-                (jnp.maximum(hi, 0.0) - jnp.minimum(lo, 0.0))
-                + (jnp.maximum(y_hi, 0.0) - jnp.minimum(y_lo, 0.0))
+            c_xm = jnp.maximum(lo, 0.0)
+            c_xp = -jnp.minimum(hi, 0.0)
+            c_ym = jnp.maximum(y_lo, 0.0)
+            c_yp = -jnp.minimum(y_hi, 0.0)
+            c_0 = (1.0 - jnp.maximum(hi, 0.0) + jnp.minimum(lo, 0.0)) - (
+                jnp.maximum(y_hi, 0.0) - jnp.minimum(y_lo, 0.0)
             )
             t_p = pltpu.roll(c_yp, NZ, axis=1)
             t_m = pltpu.roll(c_ym, NZ, axis=1)
@@ -301,6 +318,10 @@
                     + pltpu.roll(own * q + other * beside, NZ, axis=1)
                 )
                 f_ref[yb, pl.ds(r * wx + x0, half), :] = fresh
+                if part == 0:
+                    fe[0, yb, r : r + 1, :] = fresh[0:1]
+                else:
+                    fe[1, yb, r : r + 1, :] = fresh[half - 1 : half]
                 if r < MAT:
                     acc = acc + fresh * (stiff[r] + (0.5 * stiff[r]) * fresh)
                 elif r == NQ - 1:
@@ -318,8 +339,8 @@
     ]
     for e, yb in ((0, 0), (1, n_yb - 1)):
         inside = jnp.logical_not(upper) if e == 0 else upper
-        speed = 0.5 * (q_ref[yb + 1, pl.ds(row_y, wx), :] + has[e] * yr[e, NQ // 2].astype(F32))
-        speed = jnp.where(inside, TIME_STEP * speed, 0.0)
+        speed = q_ref[yb + 1, pl.ds(row_y, wx), :] + has[e] * yr[e, NQ // 2].astype(F32)
+        speed = jnp.where(inside, speed, 0.0)
         pos, neg = jnp.maximum(speed, 0.0), jnp.minimum(speed, 0.0)
         w_far, w_own = (has[e] * pos, neg) if e == 0 else (-has[e] * neg, -pos)
         acc = jnp.zeros((wx, BLK), F32)
@@ -331,6 +352,8 @@
                 rows = pl.ds(r * wx, wx)
                 fresh = f_ref[yb, rows, :] + (w_far * far + w_own * q_ref[yb + 1, rows_of(r), :])
                 f_ref[yb, rows, :] = fresh
+                fe[0, yb, r : r + 1, :] = fresh[0:1]
+                fe[1, yb, r : r + 1, :] = fresh[wx - 1 : wx]
                 if r < MAT:
                     acc = acc + fresh * (stiff[r] + (0.5 * stiff[r]) * fresh)
                 elif r == NQ - 1:
@@ -353,34 +376,33 @@
     def border_x(yb, carry):
         for e, x in ((0, 0), (1, wx - 1)):
             far = xr[e, yb].astype(F32) * has[e]
-            q = q_ref[yb + 1, pl.ds(pad + x, 16, stride=wx), :]
-            speed = (0.5 * TIME_STEP) * (q[NQ : NQ + 1] + far[NQ : NQ + 1])
+            q = xe[e, yb]
+            speed = q[NQ : NQ + 1] + far[NQ : NQ + 1]
             pos, neg = jnp.maximum(speed, 0.0), jnp.minimum(speed, 0.0)
             change = (pos * far + neg * q) if e == 0 else -(pos * q + neg * far)
             rows = pl.ds(x, 16, stride=wx)
-            fresh = f_ref[yb, rows, :] + change
+            fresh = fe[e, yb] + change
             f_ref[yb, rows, :] = fresh
             terms = jnp.where(sub16 < NQ, fresh * (lin + quad * fresh), 0.0)
             value = jnp.sum(terms, axis=0, keepdims=True)
             press[pl.ds(yb * wx + x, 1), :] = value.astype(BF16).astype(F32)
-        o_copy(yb).start()
         return carry
 
     lax.fori_loop(0, n_yb, border_x, 0)
 
-    sub48 = lax.broadcasted_iota(jnp.int32, (48, BLK), 0)
-    count = count_s[0]
+    sub24 = lax.broadcasted_iota(jnp.int32, (24, BLK), 0)
 
     def sample(i, acc):
         lefts, rights = [], []
         for g in range(group):
             t = i * group + g
-            s = jnp.where(t < count, local_slot(t), jnp.int32(100))
-            c = cell_s[t]
-            row = lax.rem(c, n_yb) * wx + c // n_yb
-            value = press[pl.ds(row, 1), :]
-            value = jnp.where(sub48 == s, jnp.broadcast_to(value, (48, BLK)), 0.0)
-            lefts.append(jnp.where(sub48 == s + 24, 1.0, value).astype(BF16))
+            hit = sub24 == loc_s[t]
+            value = jnp.broadcast_to(press[pl.ds(row_s[t], 1), :], (24, BLK))
+            lefts.append(
+                jnp.concatenate(
+                    [jnp.where(hit, value, 0.0), jnp.where(hit, 1.0, 0.0)], axis=0
+                ).astype(BF16)
+            )
             rights.append(wts[t])
         return acc + lax.dot_general(
             jnp.concatenate(lefts, axis=1), jnp.concatenate(rights, axis=1),
@@ -421,10 +443,22 @@
         c.wait_recv()
     result = jnp.dot(mine, ret[...].astype(BF16), preferred_element_type=F32)
     eo_ref[...] = result[0:n_blk]
-    for yb in range(n_yb):
-        o_copy(yb).wait()
     for c in back:
         c.wait_send()
+
+
+def write_out(n_yb, rows, f_ref, eo_ref, out_ref, ep_ref, sem):
+    copies = [
+        pltpu.make_async_copy(
+            f_ref.at[yb, pl.ds(0, rows)], out_ref.at[:, pl.ds(yb * BLK, BLK)], sem.at[yb]
+        )
+        for yb in range(n_yb)
+    ]
+    for c in copies:
+        c.start()
+    ep_ref[...] = eo_ref[...].astype(BF16)
+    for c in copies:
+        c.wait()
 
 
 def per_device(
@@ -439,21 +473,24 @@
     rows_q = 16 * wx + 16
     vmem = pl.BlockSpec(memory_space=pltpu.VMEM)
     smem = pl.BlockSpec(memory_space=pltpu.SMEM)
-    hbm = pl.BlockSpec(memory_space=pl.ANY)
+    hbm = pl.BlockSpec(memory_space=pltpu.HBM)
     dma = pltpu.SemaphoreType.DMA
-    out, eo = pl.pallas_call(
+    fresh, eo = pl.pallas_call(
         functools.partial(kernel, (gx, gy, n_blk, n_tiles, wx, n_yb)),
         out_shape=(
-            jax.ShapeDtypeStruct((NQ * wx, lanes), F32),
-            jax.ShapeDtypeStruct((n_blk, BLK), F32),
+            pltpu.VMEM((n_yb, 16 * wx, BLK), F32),
+            pltpu.VMEM((n_blk, BLK), F32),
         ),
         in_specs=[vmem] * 5 + [smem] * 5 + [hbm] * 2,
-        out_specs=(hbm, vmem),
+        out_specs=(vmem, vmem),
         scratch_shapes=[
             pltpu.VMEM((n_tiles, BLK, BLK), BF16),
             pltpu.VMEM((n_yb + 2, rows_q, BLK), F32),
-            pltpu.VMEM((n_yb, 16 * wx, BLK), F32),
-            pltpu.VMEM((16 * n_tiles, BLK), F32),
+            pltpu.VMEM((2, n_yb, 16, BLK), F32),
+            pltpu.VMEM((2, n_yb, 16, BLK), F32),
+            pltpu.SMEM((n_tiles,), jnp.int32),
+            pltpu.SMEM((n_tiles,), jnp.int32),
+            pltpu.VMEM((16 * n_tiles + 24, BLK), F32),
             pltpu.VMEM((NQ // 2, 2 * n_tiles, 2 * BLK), BF16),
             pltpu.VMEM((n_yb * wx, BLK), F32),
             pltpu.VMEM((n_blk, 16, BLK), F32),
@@ -465,11 +502,11 @@
             pltpu.VMEM((2, NQ // 2 + 1, wx, BLK), BF16),
             pltpu.VMEM((128, BLK), F32),
             pltpu.VMEM((128, BLK), F32),
-            dma((4,)), dma((n_yb,)), dma((n_yb,)),
+            dma((4,)), dma((n_yb,)),
             dma((8,)), dma((8,)), dma((2,)), dma((2,)), dma((2,)), dma((2,)), dma((8,)), dma((8,)),
         ],
         compiler_params=pltpu.CompilerParams(
-            collective_id=0, has_side_effects=True, vmem_limit_bytes=56 * 1024 * 1024
+            collective_id=0, has_side_effects=True, vmem_limit_bytes=67043328 - 8388608 - 16384
         ),
     )(
         elem_volume.reshape(n_blk, BLK), elem_velocity, elem_energy.reshape(n_blk, BLK),
@@ -477,7 +514,18 @@
         elem_dest, tile_slot, tile_cell, tile_count, mat_props,
         tile_weight, cell_state.reshape(NQ * wx, lanes),
     )
-    return out.reshape(NQ, wx, lanes), eo.astype(BF16).reshape(n_blk * BLK)
+    out, pressure = pl.pallas_call(
+        functools.partial(write_out, n_yb, NQ * wx),
+        out_shape=(
+            jax.ShapeDtypeStruct((NQ * wx, lanes), F32),
+            jax.ShapeDtypeStruct((n_blk, BLK), BF16),
+        ),
+        in_specs=[vmem, vmem],
+        out_specs=(hbm, vmem),
+        scratch_shapes=[dma((n_yb,))],
+        compiler_params=pltpu.CompilerParams(vmem_limit_bytes=4 * 1024 * 1024),
+    )(fresh, eo)
+    return out.reshape(NQ, wx, lanes), pressure.reshape(n_blk * BLK)
 
 
 def solution(mesh):

time: 49.9 us -> 38.1 us (0.76)
  local copies, waits for them, and re-layouts: 6.28 us -> 0 us
  Pallas kernels: 40.7 us -> 36.6 us
  other arithmetic: 1.3 us -> 0 us
    pallas_call x1, Pallas kernels: 40.7 us -> 33.3 us  [per_device(): pl.pallas_call(functools.partial(kernel, (gx, gy, n_blk, n_tiles, wx, n_y...]
    unnamed x1 -> x0, local copies, waits for them, and re-layouts: 6.28 us -> none
    pallas_call x0 -> x1, Pallas kernels: none -> 3.37 us  [per_device(): pl.pallas_call(functools.partial(write_out, n_yb, NQ * wx), out_shape=(ja...]
    reshape x1 -> x0, other arithmetic: 1.3 us -> none  [per_device(): return (out.reshape(NQ, wx, lanes), eo.astype(BF16).reshape(n_blk * BLK))]
where the time goes in v2:
time: 38.1 us; the launch traced here: 37.9 us
  Pallas kernels  36.6 us (96%)
  between operations  1.29 us (3%)
    pallas_call x1, Pallas kernels, per_device(): pl.pallas_call(functools.partial(kernel, (gx, gy, n_blk, n_tiles, wx, n_y...  33.3 us
    pallas_call x1, Pallas kernels, per_device(): pl.pallas_call(functools.partial(write_out, n_yb, NQ * wx), out_shape=(ja...  3.37 us

profile of v2, /device:TPU:0, one launch (start us, length us, event | category | flops | bytes accessed | tf_op | source)
XLA Modules:
  0.0 37.9 jit_solution(4627436719529945482)
XLA Ops:
  1.3 33.3 %shard_map.122 = (f32[16,1024,128]{2,1,0:T(8,128)S(1)}, f32[18,128]{1,0:T(8,128)S(1)}) custom-call(f32[18,128]{1,0:T(8,128)} %bitcast.8, f32[3,2304]{1,0:T(4,128)} %vel.1, f32[18,128]{1,0:T(8,128)} %bitcast.9, s32[18,128]{1,0:T(8,128)} %bitcast.10, s32[1,128]{1,0:T(1,128)} %bitcast.11, s32[18]{0:T(128)} %dest_s.1, s32[128]{0:T(128)} %slot_s.1, s32[128]{0:T(128)} %cell_s.1, ...), custom_call_target="tpu_custom_call" | custom-call | tf_op jit(solution)/shard_map/pallas_call | solution.py:478
  34.5 3.4 %shard_map.123 = (f32[768,2048]{1,0:T(8,128)}, bf16[18,128]{1,0:T(8,128)(2,1)}) custom-call(f32[16,1024,128]{2,1,0:T(8,128)S(1)} %get-tuple-element.6.f_ref, f32[18,128]{1,0:T(8,128)S(1)} %get-tuple-element.7.eo_ref), custom_call_target="tpu_custom_call" | custom-call | tf_op jit(solution)/shard_map/pallas_call | solution.py:517

commit v3 on v2

--- a/solution.py
+++ b/solution.py
@@ -22,10 +22,11 @@
 
 def kernel(
     dims,
-    vol, vel, ene, mat, cell_v, dest_s, slot_s, cell_s, count_s, props_s, w_hbm, state_hbm,
+    vol_h, vel_h, ene_h, mat_h, cell_h, dest_h, slot_h, cell1_h, count_h, props_h, w_hbm, state_hbm,
     f_ref, eo_ref,
-    wts, q_ref, xe, fe, loc_s, row_s, s_ref, c_ref, press, blk, outg, recv, xs, xr, ys, yr, anss, ret,
-    w_sem, q_sem, pay_s, pay_r, hx_s, hx_r, hy_s, hy_r, ret_s, ret_r,
+    vol, vel, ene, mat, cell_v, dest_s, slot_s, cell_s, count_s, props_s,
+    wts, q_ref, xe, fe, at_s, loc_s, row_s, s_ref, c_ref, press, blk, outg, recv, xs, xr, ys, yr, anss, ret,
+    in_sem, w_sem, q_sem, pay_s, pay_r, hx_s, hx_r, hy_s, hy_r, ret_s, ret_r,
 ):
     gx, gy, n_blk, n_tiles, wx, n_yb = dims
     px = lax.axis_index("gx")
@@ -59,8 +60,19 @@
     for a, b in NEAR:
         if (a, b) != (1, 1):
             pl.semaphore_signal(barrier, inc=1, device_id=dev(a, b, 1), device_id_type=MESH)
+    small = [
+        pltpu.make_async_copy(src, dst, in_sem.at[i])
+        for i, (src, dst) in enumerate((
+            (dest_h, dest_s), (props_h, props_s), (vol_h, vol), (mat_h, mat), (vel_h, vel),
+            (ene_h, ene), (slot_h, slot_s), (cell1_h, cell_s), (count_h, count_s), (cell_h, cell_v),
+        ))
+    ]
+    for c in small:
+        c.start()
     for i in range(n_chunk):
         w_copy(i).start()
+    for c in small:
+        c.wait()
 
     sub8 = lax.broadcasted_iota(jnp.int32, (8, BLK), 0)
     dens = [props_s[0, m] for m in range(MAT)]
@@ -148,27 +160,32 @@
 
     lax.fori_loop(0, n_yb, clear_edge, 0)
 
+    count = count_s[0]
+
+    def places(i, carry):
+        for g in range(8):
+            t = i * 8 + g
+            s = slot_s[t]
+            a = (px + 1 - (s >> (bits_y + 1))) & (gx - 1)
+            b = (py + 1 - (s >> 1)) & (gy - 1)
+            at = jnp.minimum(a * 6 + b * 2 + (s & 1), n_blk - 1)
+            at_s[t] = at
+            loc_s[t] = jnp.where(t < count, at, jnp.int32(100))
+            cell = cell_s[t]
+            row_s[t] = ((cell & (n_yb - 1)) << bits_x) + (cell >> bits_b)
+        return carry
+
+    lax.fori_loop(0, n_tiles // 8, places, 0)
+
     for c in pay:
         c.wait_recv()
     for i in range(n_chunk):
         w_copy(i).wait()
 
-    count = count_s[0]
-
-    def local_slot(t):
-        s = slot_s[t]
-        a = (px + 1 - (s >> (bits_y + 1))) & (gx - 1)
-        b = (py + 1 - (s >> 1)) & (gy - 1)
-        return jnp.minimum(a * 6 + b * 2 + (s & 1), n_blk - 1)
-
     def contrib(i, carry):
         for g in range(group):
             t = i * group + g
-            at = local_slot(t)
-            loc_s[t] = jnp.where(t < count, at, jnp.int32(100))
-            cell = cell_s[t]
-            row_s[t] = ((cell & (n_yb - 1)) << bits_x) + (cell >> bits_b)
-            c = jnp.dot(recv[at], wts[t], preferred_element_type=F32)
+            c = jnp.dot(recv[at_s[t]], wts[t], preferred_element_type=F32)
             s_ref[pl.ds(t, 16, stride=pitch), :] = c
         return carry
 
@@ -269,13 +286,15 @@
         )
         halo[-1].start()
 
-    half = wx // 2
+    parts = 2
+    half = wx // parts
     sub = lax.broadcasted_iota(jnp.int32, (half, BLK), 0)
     lane_h = lax.broadcasted_iota(jnp.int32, (half, BLK), 1)
     upper_h = lane_h >= NZ
 
     def remap(yb, carry):
-        for part in range(2):
+        lanes = pl.ds(pl.multiple_of(yb * BLK, BLK), BLK)
+        for part in range(parts):
             x0 = part * half
 
             def at(base, shift=0):
@@ -286,7 +305,7 @@
             hi = ux + q_ref[yb + 1, at(row_x, 1), :]
             if part == 0:
                 lo = jnp.where(sub == 0, 0.0, lo)
-            else:
+            elif part == parts - 1:
                 hi = jnp.where(sub == half - 1, 0.0, hi)
             uy = q_ref[yb + 1, at(row_y), :]
             prev, after = q_ref[yb, at(row_y), :], q_ref[yb + 2, at(row_y), :]
@@ -317,10 +336,10 @@
                     + c_xp * q_ref[yb + 1, at(base, 1), :]
                     + pltpu.roll(own * q + other * beside, NZ, axis=1)
                 )
-                f_ref[yb, pl.ds(r * wx + x0, half), :] = fresh
+                f_ref[pl.ds(r * wx + x0, half), lanes] = fresh
                 if part == 0:
                     fe[0, yb, r : r + 1, :] = fresh[0:1]
-                else:
+                elif part == parts - 1:
                     fe[1, yb, r : r + 1, :] = fresh[half - 1 : half]
                 if r < MAT:
                     acc = acc + fresh * (stiff[r] + (0.5 * stiff[r]) * fresh)
@@ -349,9 +368,9 @@
             for h in range(2):
                 r = 2 * p + h
                 far = packed if h == 0 else pltpu.roll(packed, NZ, axis=1)
-                rows = pl.ds(r * wx, wx)
-                fresh = f_ref[yb, rows, :] + (w_far * far + w_own * q_ref[yb + 1, rows_of(r), :])
-                f_ref[yb, rows, :] = fresh
+                here = (slice(r * wx, (r + 1) * wx), slice(yb * BLK, (yb + 1) * BLK))
+                fresh = f_ref[here] + (w_far * far + w_own * q_ref[yb + 1, rows_of(r), :])
+                f_ref[here] = fresh
                 fe[0, yb, r : r + 1, :] = fresh[0:1]
                 fe[1, yb, r : r + 1, :] = fresh[wx - 1 : wx]
                 if r < MAT:
@@ -373,22 +392,24 @@
         jnp.where(px < gx - 1, 1.0, 0.0).astype(F32),
     ]
 
-    def border_x(yb, carry):
-        for e, x in ((0, 0), (1, wx - 1)):
-            far = xr[e, yb].astype(F32) * has[e]
-            q = xe[e, yb]
-            speed = q[NQ : NQ + 1] + far[NQ : NQ + 1]
-            pos, neg = jnp.maximum(speed, 0.0), jnp.minimum(speed, 0.0)
-            change = (pos * far + neg * q) if e == 0 else -(pos * q + neg * far)
-            rows = pl.ds(x, 16, stride=wx)
-            fresh = fe[e, yb] + change
-            f_ref[yb, rows, :] = fresh
-            terms = jnp.where(sub16 < NQ, fresh * (lin + quad * fresh), 0.0)
-            value = jnp.sum(terms, axis=0, keepdims=True)
-            press[pl.ds(yb * wx + x, 1), :] = value.astype(BF16).astype(F32)
-        return carry
-
-    lax.fori_loop(0, n_yb, border_x, 0)
+    def border_x(i, carry):
+        for yb in (2 * i, 2 * i + 1):
+            lanes = pl.ds(pl.multiple_of(yb * BLK, BLK), BLK)
+            for e, x in ((0, 0), (1, wx - 1)):
+                far = xr[e, yb].astype(F32) * has[e]
+                q = xe[e, yb]
+                speed = q[NQ : NQ + 1] + far[NQ : NQ + 1]
+                pos, neg = jnp.maximum(speed, 0.0), jnp.minimum(speed, 0.0)
+                change = (pos * far + neg * q) if e == 0 else -(pos * q + neg * far)
+                fresh = fe[e, yb] + change
+                for r in range(NQ):
+                    f_ref[r * wx + x : r * wx + x + 1, lanes] = fresh[r : r + 1]
+                terms = jnp.where(sub16 < NQ, fresh * (lin + quad * fresh), 0.0)
+                value = jnp.sum(terms, axis=0, keepdims=True)
+                press[pl.ds(yb * wx + x, 1), :] = value.astype(BF16).astype(F32)
+        return carry
+
+    lax.fori_loop(0, n_yb // 2, border_x, 0)
 
     sub24 = lax.broadcasted_iota(jnp.int32, (24, BLK), 0)
 
@@ -447,12 +468,11 @@
         c.wait_send()
 
 
-def write_out(n_yb, rows, f_ref, eo_ref, out_ref, ep_ref, sem):
+def write_out(f_ref, eo_ref, out_ref, ep_ref, sem):
+    step = f_ref.shape[0] // sem.shape[0]
     copies = [
-        pltpu.make_async_copy(
-            f_ref.at[yb, pl.ds(0, rows)], out_ref.at[:, pl.ds(yb * BLK, BLK)], sem.at[yb]
-        )
-        for yb in range(n_yb)
+        pltpu.make_async_copy(f_ref.at[pl.ds(i * step, step)], out_ref.at[pl.ds(i * step, step)], sem.at[i])
+        for i in range(sem.shape[0])
     ]
     for c in copies:
         c.start()
@@ -472,24 +492,26 @@
     n_yb = lanes // BLK
     rows_q = 16 * wx + 16
     vmem = pl.BlockSpec(memory_space=pltpu.VMEM)
-    smem = pl.BlockSpec(memory_space=pltpu.SMEM)
+    smem, i32 = pltpu.SMEM, jnp.int32
     hbm = pl.BlockSpec(memory_space=pltpu.HBM)
     dma = pltpu.SemaphoreType.DMA
     fresh, eo = pl.pallas_call(
         functools.partial(kernel, (gx, gy, n_blk, n_tiles, wx, n_yb)),
         out_shape=(
-            pltpu.VMEM((n_yb, 16 * wx, BLK), F32),
+            pltpu.VMEM((NQ * wx, lanes), F32),
             pltpu.VMEM((n_blk, BLK), F32),
         ),
-        in_specs=[vmem] * 5 + [smem] * 5 + [hbm] * 2,
+        in_specs=[hbm] * 12,
         out_specs=(vmem, vmem),
         scratch_shapes=[
+            pltpu.VMEM((n_blk, BLK), F32), pltpu.VMEM((3, n_blk * BLK), F32),
+            pltpu.VMEM((n_blk, BLK), F32), pltpu.VMEM((n_blk, BLK), i32), pltpu.VMEM((1, n_tiles), i32),
+            smem((n_blk,), i32), smem((n_tiles,), i32), smem((n_tiles,), i32), smem((1,), i32), smem((2, MAT), F32),
             pltpu.VMEM((n_tiles, BLK, BLK), BF16),
             pltpu.VMEM((n_yb + 2, rows_q, BLK), F32),
             pltpu.VMEM((2, n_yb, 16, BLK), F32),
             pltpu.VMEM((2, n_yb, 16, BLK), F32),
-            pltpu.SMEM((n_tiles,), jnp.int32),
-            pltpu.SMEM((n_tiles,), jnp.int32),
+            smem((n_tiles,), i32), smem((n_tiles,), i32), smem((n_tiles,), i32),
             pltpu.VMEM((16 * n_tiles + 24, BLK), F32),
             pltpu.VMEM((NQ // 2, 2 * n_tiles, 2 * BLK), BF16),
             pltpu.VMEM((n_yb * wx, BLK), F32),
@@ -502,11 +524,11 @@
             pltpu.VMEM((2, NQ // 2 + 1, wx, BLK), BF16),
             pltpu.VMEM((128, BLK), F32),
             pltpu.VMEM((128, BLK), F32),
-            dma((4,)), dma((n_yb,)),
+            dma((10,)), dma((4,)), dma((n_yb,)),
             dma((8,)), dma((8,)), dma((2,)), dma((2,)), dma((2,)), dma((2,)), dma((8,)), dma((8,)),
         ],
         compiler_params=pltpu.CompilerParams(
-            collective_id=0, has_side_effects=True, vmem_limit_bytes=67043328 - 8388608 - 16384
+            collective_id=0, has_side_effects=True, vmem_limit_bytes=67043328 - 6291456 - 16384
         ),
     )(
         elem_volume.reshape(n_blk, BLK), elem_velocity, elem_energy.reshape(n_blk, BLK),
@@ -515,14 +537,14 @@
         tile_weight, cell_state.reshape(NQ * wx, lanes),
     )
     out, pressure = pl.pallas_call(
-        functools.partial(write_out, n_yb, NQ * wx),
+        write_out,
         out_shape=(
             jax.ShapeDtypeStruct((NQ * wx, lanes), F32),
             jax.ShapeDtypeStruct((n_blk, BLK), BF16),
         ),
         in_specs=[vmem, vmem],
         out_specs=(hbm, vmem),
-        scratch_shapes=[dma((n_yb,))],
+        scratch_shapes=[dma((8,))],
         compiler_params=pltpu.CompilerParams(vmem_limit_bytes=4 * 1024 * 1024),
     )(fresh, eo)
     return out.reshape(NQ, wx, lanes), pressure.reshape(n_blk * BLK)

time: 38.1 us -> 37 us (0.971)
  Pallas kernels: 36.6 us -> 35.6 us
    pallas_call x1, Pallas kernels: 33.3 us -> 32.3 us  [per_device(): pl.pallas_call(functools.partial(kernel, (gx, gy, n_blk, n_tiles, wx, n_y...]
where the time goes in v3:
time: 37 us; the launch traced here: 36.9 us
  Pallas kernels  35.6 us (96%)
  between operations  1.29 us (3%)
    pallas_call x1, Pallas kernels, per_device(): pl.pallas_call(functools.partial(kernel, (gx, gy, n_blk, n_tiles, wx, n_y...  32.3 us
    pallas_call x1, Pallas kernels, per_device(): pl.pallas_call(write_out, out_shape=(jax.ShapeDtypeStruct((NQ * wx, lanes...  3.33 us

profile of v3, /device:TPU:0, one launch (start us, length us, event | category | flops | bytes accessed | tf_op | source)
XLA Modules:
  0.0 36.9 jit_solution(614104625894786850)
XLA Ops:
  1.3 32.3 %shard_map.122 = (f32[768,2048]{1,0:T(8,128)S(1)}, f32[18,128]{1,0:T(8,128)S(1)}) custom-call(f32[18,128]{1,0:T(8,128)} %bitcast.8, f32[3,2304]{1,0:T(4,128)} %vel_h.1, f32[18,128]{1,0:T(8,128)} %bitcast.9, s32[18,128]{1,0:T(8,128)} %bitcast.10, s32[1,128]{1,0:T(1,128)} %bitcast.11, s32[18]{0:T(128)} %dest_h.1, s32[128]{0:T(128)} %slot_h.1, s32[128]{0:T(128)} %cell1_h.1, ...), custom_call_target="tpu_custom_call" | custom-call | tf_op jit(solution)/shard_map/pallas_call | solution.py:498
  33.6 3.3 %shard_map.123 = (f32[768,2048]{1,0:T(8,128)}, bf16[18,128]{1,0:T(8,128)(2,1)}) custom-call(f32[768,2048]{1,0:T(8,128)S(1)} %get-tuple-element.6.f_ref, f32[18,128]{1,0:T(8,128)S(1)} %get-tuple-element.7.eo_ref), custom_call_target="tpu_custom_call" | custom-call | tf_op jit(solution)/shard_map/pallas_call | solution.py:539

commit v4 on v3

--- a/solution.py
+++ b/solution.py
@@ -154,7 +154,6 @@
 
     def clear_edge(yb, carry):
         for e in range(2):
-            xe[e, yb] = jnp.zeros((16, BLK), F32)
             fe[e, yb] = jnp.zeros((16, BLK), F32)
         return carry
 
@@ -182,41 +181,41 @@
     for i in range(n_chunk):
         w_copy(i).wait()
 
+    def gather(i):
+        at = pl.multiple_of(i * group, group)
+        for r in range(NQ):
+            value = s_ref[pl.ds(r * pitch + at, group), :]
+            c_ref[r // 2, pl.ds(at, group), (r % 2) * BLK : (r % 2 + 1) * BLK] = value.astype(BF16)
+
     def contrib(i, carry):
-        for g in range(group):
+        gather(jnp.maximum(i - 1, 0))
+        for g in range(0, group, 2):
             t = i * group + g
-            c = jnp.dot(recv[at_s[t]], wts[t], preferred_element_type=F32)
-            s_ref[pl.ds(t, 16, stride=pitch), :] = c
+            left = jnp.concatenate([recv[at_s[t]], recv[at_s[t + 1]]], axis=0)
+            right = jnp.concatenate([wts[t], wts[t + 1]], axis=1)
+            c = jnp.dot(left, right, preferred_element_type=F32)
+            s_ref[pl.ds(t, 16, stride=pitch), :] = c[0:16, 0:BLK]
+            s_ref[pl.ds(t + 1, 16, stride=pitch), :] = c[16:32, BLK : 2 * BLK]
         return carry
 
     lax.fori_loop(0, n_tiles // group, contrib, 0)
-
-    for p in range(NQ // 2):
-        for h in range(2):
-            value = s_ref[pl.ds((2 * p + h) * pitch, n_tiles), :]
-            high = value.astype(BF16)
-            c_ref[p, 0:n_tiles, h * BLK : (h + 1) * BLK] = high
-            c_ref[p, n_tiles : 2 * n_tiles, h * BLK : (h + 1) * BLK] = (
-                value - high.astype(F32)
-            ).astype(BF16)
+    gather(n_tiles // group - 1)
 
     lane_t = lax.broadcasted_iota(jnp.int32, (1, n_tiles), 1)
     cell_m = jnp.broadcast_to(jnp.where(lane_t < count, cell_v[...], -1), (wx, n_tiles))
     cell_at = lax.broadcasted_iota(jnp.int32, (wx, n_tiles), 0) * n_yb
 
-    def deposit(one, two):
+    def deposit(blocks):
         picks = []
-        for yb in (one, two):
+        for yb in blocks:
             q_copy(yb).wait()
             picks.append(jnp.where(cell_m == cell_at + yb, 1.0, 0.0).astype(BF16))
-        left = jnp.concatenate(
-            [jnp.concatenate([pick, pick], axis=1) for pick in picks], axis=0
-        )
-        mass = [jnp.ones((wx, BLK), F32) for _ in range(2)]
-        moving = [[], []]
+        left = jnp.concatenate(picks, axis=0)
+        mass = [jnp.ones((wx, BLK), F32) for _ in blocks]
+        moving = [[] for _ in blocks]
         for p in range(NQ // 2):
             both = jnp.dot(left, c_ref[p], preferred_element_type=F32)
-            for k, yb in enumerate((one, two)):
+            for k, yb in enumerate(blocks):
                 for h in range(2):
                     r = 2 * p + h
                     rows = pl.ds(pad + r * wx, wx)
@@ -225,23 +224,22 @@
                         + both[k * wx : (k + 1) * wx, h * BLK : (h + 1) * BLK]
                     )
                     q_ref[yb + 1, rows, :] = value
-                    xe[0, yb, r : r + 1, :] = value[0:1]
-                    xe[1, yb, r : r + 1, :] = value[wx - 1 : wx]
                     if r < MAT:
                         mass[k] = mass[k] + dens[r] * value
                     elif r < MAT + 2:
                         moving[k].append(value)
-        for k, yb in enumerate((one, two)):
+        for k, yb in enumerate(blocks):
             scale = (0.5 * TIME_STEP) / mass[k]
             u = moving[k][0] * scale
             q_ref[yb + 1, pl.ds(row_x, wx), :] = u
             q_ref[yb + 1, pl.ds(row_y, wx), :] = moving[k][1] * scale
-            xe[0, yb, NQ : NQ + 1, :] = u[0:1]
-            xe[1, yb, NQ : NQ + 1, :] = u[wx - 1 : wx]
-            for e in range(2):
-                xs[e, yb] = xe[e, yb].astype(BF16)
-
-    deposit(0, n_yb - 1)
+        for yb in blocks:
+            for e, x in ((0, 0), (1, wx - 1)):
+                edge = q_ref[yb + 1, pl.ds(pad + x, 16, stride=wx), :]
+                xe[e, yb] = edge
+                xs[e, yb] = edge.astype(BF16)
+
+    deposit((0, n_yb - 1, 1, 2))
 
     lane = lax.broadcasted_iota(jnp.int32, (wx, BLK), 1)
     upper = lane >= NZ
@@ -272,10 +270,10 @@
         halo[-1].start()
 
     def deposit_inner(i, carry):
-        deposit(2 * i + 1, 2 * i + 2)
-        return carry
-
-    lax.fori_loop(0, n_yb // 2 - 1, deposit_inner, 0)
+        deposit(tuple(4 * i + 3 + k for k in range(4)))
+        return carry
+
+    lax.fori_loop(0, n_yb // 4 - 1, deposit_inner, 0)
 
     for e, a in ((0, 0), (1, 2)):
         halo.append(
@@ -413,10 +411,12 @@
 
     sub24 = lax.broadcasted_iota(jnp.int32, (24, BLK), 0)
 
+    many = 2 * group
+
     def sample(i, acc):
         lefts, rights = [], []
-        for g in range(group):
-            t = i * group + g
+        for g in range(many):
+            t = i * many + g
             hit = sub24 == loc_s[t]
             value = jnp.broadcast_to(press[pl.ds(row_s[t], 1), :], (24, BLK))
             lefts.append(
@@ -430,7 +430,7 @@
             (((1,), (1,)), ((), ())), preferred_element_type=F32,
         )
 
-    acc = lax.fori_loop(0, n_tiles // group, sample, jnp.zeros((48, BLK), F32))
+    acc = lax.fori_loop(0, n_tiles // many, sample, jnp.zeros((48, BLK), F32))
     answer = (acc[0:24] / jnp.maximum(acc[24:48], 1.0)).astype(BF16).astype(F32)
 
     back = []
@@ -513,7 +513,7 @@
             pltpu.VMEM((2, n_yb, 16, BLK), F32),
             smem((n_tiles,), i32), smem((n_tiles,), i32), smem((n_tiles,), i32),
             pltpu.VMEM((16 * n_tiles + 24, BLK), F32),
-            pltpu.VMEM((NQ // 2, 2 * n_tiles, 2 * BLK), BF16),
+            pltpu.VMEM((NQ // 2, n_tiles, 2 * BLK), BF16),
             pltpu.VMEM((n_yb * wx, BLK), F32),
             pltpu.VMEM((n_blk, 16, BLK), F32),
             pltpu.VMEM((n_blk, 16, BLK), BF16),

time: 37 us -> 35.6 us (0.962)
  Pallas kernels: 35.6 us -> 34.2 us
    pallas_call x1, Pallas kernels: 32.3 us -> 30.8 us  [per_device(): pl.pallas_call(functools.partial(kernel, (gx, gy, n_blk, n_tiles, wx, n_y...]
where the time goes in v4:
time: 35.6 us; the launch traced here: 35.4 us
  Pallas kernels  34.2 us (96%)
  between operations  1.29 us (4%)
    pallas_call x1, Pallas kernels, per_device(): pl.pallas_call(functools.partial(kernel, (gx, gy, n_blk, n_tiles, wx, n_y...  30.8 us
    pallas_call x1, Pallas kernels, per_device(): pl.pallas_call(write_out, out_shape=(jax.ShapeDtypeStruct((NQ * wx, lanes...  3.33 us

profile of v4, /device:TPU:0, one launch (start us, length us, event | category | flops | bytes accessed | tf_op | source)
XLA Modules:
  0.0 35.4 jit_solution(12014051462147209604)
XLA Ops:
  1.3 30.8 %shard_map.122 = (f32[768,2048]{1,0:T(8,128)S(1)}, f32[18,128]{1,0:T(8,128)S(1)}) custom-call(f32[18,128]{1,0:T(8,128)} %bitcast.8, f32[3,2304]{1,0:T(4,128)} %vel_h.1, f32[18,128]{1,0:T(8,128)} %bitcast.9, s32[18,128]{1,0:T(8,128)} %bitcast.10, s32[1,128]{1,0:T(1,128)} %bitcast.11, s32[18]{0:T(128)} %dest_h.1, s32[128]{0:T(128)} %slot_h.1, s32[128]{0:T(128)} %cell1_h.1, ...), custom_call_target="tpu_custom_call" | custom-call | tf_op jit(solution)/shard_map/pallas_call | solution.py:498
  32.1 3.3 %shard_map.123 = (f32[768,2048]{1,0:T(8,128)}, bf16[18,128]{1,0:T(8,128)(2,1)}) custom-call(f32[768,2048]{1,0:T(8,128)S(1)} %get-tuple-element.6.f_ref, f32[18,128]{1,0:T(8,128)S(1)} %get-tuple-element.7.eo_ref), custom_call_target="tpu_custom_call" | custom-call | tf_op jit(solution)/shard_map/pallas_call | solution.py:539

commit v5 on v4

--- a/solution.py
+++ b/solution.py
@@ -69,10 +69,10 @@
     ]
     for c in small:
         c.start()
+    for c in small[:6]:
+        c.wait()
     for i in range(n_chunk):
         w_copy(i).start()
-    for c in small:
-        c.wait()
 
     sub8 = lax.broadcasted_iota(jnp.int32, (8, BLK), 0)
     dens = [props_s[0, m] for m in range(MAT)]
@@ -159,6 +159,8 @@
 
     lax.fori_loop(0, n_yb, clear_edge, 0)
 
+    for c in small[6:]:
+        c.wait()
     count = count_s[0]
 
     def places(i, carry):
@@ -288,10 +290,10 @@
     half = wx // parts
     sub = lax.broadcasted_iota(jnp.int32, (half, BLK), 0)
     lane_h = lax.broadcasted_iota(jnp.int32, (half, BLK), 1)
-    upper_h = lane_h >= NZ
 
     def remap(yb, carry):
         lanes = pl.ds(pl.multiple_of(yb * BLK, BLK), BLK)
+        upper_h = lane_h >= NZ + jnp.minimum(yb, 0)
         for part in range(parts):
             x0 = part * half
 

time: 35.6 us -> 35.5 us (level)
  no operation moved by 1% of the time
where the time goes in v5:
time: 35.5 us; the launch traced here: 35.4 us
  Pallas kernels  34.1 us (96%)
  between operations  1.29 us (4%)
    pallas_call x1, Pallas kernels, per_device(): pl.pallas_call(functools.partial(kernel, (gx, gy, n_blk, n_tiles, wx, n_y...  30.7 us
    pallas_call x1, Pallas kernels, per_device(): pl.pallas_call(write_out, out_shape=(jax.ShapeDtypeStruct((NQ * wx, lanes...  3.33 us

profile of v5, /device:TPU:0, one launch (start us, length us, event | category | flops | bytes accessed | tf_op | source)
XLA Modules:
  0.0 35.4 jit_solution(1164118167777088838)
XLA Ops:
  1.3 30.7 %shard_map.122 = (f32[768,2048]{1,0:T(8,128)S(1)}, f32[18,128]{1,0:T(8,128)S(1)}) custom-call(f32[18,128]{1,0:T(8,128)} %bitcast.8, f32[3,2304]{1,0:T(4,128)} %vel_h.1, f32[18,128]{1,0:T(8,128)} %bitcast.9, s32[18,128]{1,0:T(8,128)} %bitcast.10, s32[1,128]{1,0:T(1,128)} %bitcast.11, s32[18]{0:T(128)} %dest_h.1, s32[128]{0:T(128)} %slot_h.1, s32[128]{0:T(128)} %cell1_h.1, ...), custom_call_target="tpu_custom_call" | custom-call | tf_op jit(solution)/shard_map/pallas_call | solution.py:500
  32.0 3.3 %shard_map.123 = (f32[768,2048]{1,0:T(8,128)}, bf16[18,128]{1,0:T(8,128)(2,1)}) custom-call(f32[768,2048]{1,0:T(8,128)S(1)} %get-tuple-element.6.f_ref, f32[18,128]{1,0:T(8,128)S(1)} %get-tuple-element.7.eo_ref), custom_call_target="tpu_custom_call" | custom-call | tf_op jit(solution)/shard_map/pallas_call | solution.py:541
